TPU v7x, 32 devices: a whole 2x2x4 slice. The times are simulated.
32 devices in a mesh: occ: 4 (over x, core), vir: 8 (over z, y).
Axes of the slice: x: 2, y: 2, z: 4, core: 2. Of those that a mesh axis runs over, the one named last changes fastest.
Arguments:
- amps: bfloat16 [4096, 3072], P('occ', 'vir'), may hold values from -6 to 6
- ints: bfloat16 [3072, 4096], P(None, 'vir'), may hold values from -0.109375 to 0.109375
- amp_mask: int32 [128, 6], P('occ'), may hold values 0 or 1
- keep_mask: int32 [128, 8], P('occ', 'vir'), may hold values 0 or 1
- owners: int32 [128, 1], P('occ'), may hold values from 0 to 3; in each aligned block of 32 rows (0 to 31, 32 to 63, ...) at most 16 rows name the same one
- occ_energy: bfloat16 [4096], P('occ'), may hold values from -2 to -0.5
- vir_energy: float32 [4096], P('vir'), may hold values from 0.5 to 3
- mix: bfloat16 [4, 32, 32], P('occ'), may hold values from -4 to 4
Outputs:
- owned: bfloat16 [256, 32, 4096], P('occ', None, 'vir')
Inputs may be any that keep to these rules, and one draw needn't show every extreme that they name: `owners`: in the row tiles of one index of occ no owner appears more than 16 times; in every draw some owner appears exactly 16 times in some device's tiles.
All inputs are finite; a program needn't handle non-finite values. No bound on the sum of `amp_mask` or of `keep_mask` on one device may be relied on, other than what follows from the above.
Results may differ from a plain program's by a relative error of at most 0.0049.
Values may be sent and summed in bfloat16 or wider, within the bound.
A program may use at most 64 MiB of HBM per device.

v0:
```python
import functools

import jax
import jax.numpy as jnp
from jax import lax
from jax.experimental import pallas as pl
from jax.experimental.pallas import tpu as pltpu
from jax.sharding import PartitionSpec as P

MESH = pl.DeviceIdType.MESH


def ladder_kernel(
    cfg, amps, ints, amp_mask, keep, own_s, own_v, occ, vir, mix, out,
    gath, ints_v, occ_col, tiles, mix_all, own_all, own_tab, nxt,
    lsem, rsem_g, ssem_g, rsem_t, ssem_c, ssem_t, rsem_o, ssem_o,
):
    no, nv, td, tr, chunk_tiles, k_tile, ahead, ahead_side, stagger, lag, side_every = cfg
    ng, nz = no // 2, nv // 2
    rows, kw = amps.shape
    cols = ints.shape[1]
    cr = chunk_tiles * tr
    nc = rows // cr
    cap = out.shape[0] // no
    o, v = lax.axis_index("occ"), lax.axis_index("vir")
    g, c = o // 2, o % 2
    z, y = v // 2, v % 2
    partner = {"occ": g * 2 + (1 - c), "vir": v}
    side = {"occ": o, "vir": z * 2 + (1 - y)}
    above = {"occ": o, "vir": (z + 1) * 2 + y}
    below = {"occ": o, "vir": (z - 1) * 2 + y}

    local = [
        pltpu.make_async_copy(own_v, own_all.at[o], lsem.at[0]),
        pltpu.make_async_copy(ints, ints_v, lsem.at[3]),
        pltpu.make_async_copy(mix.at[0], mix_all.at[o], lsem.at[1]),
    ]
    for copy in local:
        copy.start()

    barrier = pltpu.get_barrier_semaphore()

    def greet(device):
        pl.semaphore_signal(barrier, inc=1, device_id=device, device_id_type=MESH)

    for d in range(1, no):
        greet({"occ": (o + d) % no, "vir": v})
    greet(side)

    @pl.when(z < nz - 1)
    def _():
        greet(above)

    @pl.when(z > 0)
    def _():
        greet(below)

    inner = jnp.where(z < nz - 1, 1, 0) + jnp.where(z > 0, 1, 0)
    pl.semaphore_wait(barrier, no + inner)

    def piece(src, slot, i, send_sem, device):
        window = pl.ds(pl.multiple_of(i * cr, cr), cr)
        return pltpu.make_async_remote_copy(
            src_ref=src.at[window], dst_ref=gath.at[slot, window], send_sem=send_sem,
            recv_sem=rsem_g.at[slot, i], device_id=device, device_id_type=MESH,
        )

    def side_first(i):
        return i % side_every == side_every // 2

    def spread(src, slot, i, up, down, across):
        if up:
            @pl.when(z < nz - 1)
            def _():
                piece(src, slot, i, ssem_g.at[0, slot], above).start()
        if down:
            @pl.when(z > 0)
            def _():
                piece(src, slot, i, ssem_g.at[1, slot], below).start()
        if across:
            piece(src, slot, i, ssem_g.at[2, slot], side).start()

    def arrive(slot, i):
        piece(gath.at[slot], slot, i, ssem_g.at[2, 0], side).wait_recv()

    for i in range(min(ahead_side, nc)):
        if i < ahead:
            spread(amps, v, i, True, True, False)
        spread(amps, v, i, False, False, True)

    def small(d, o2):
        peer = {"occ": (o + d) % no, "vir": v}
        return [
            pltpu.make_async_remote_copy(
                src_ref=own_v, dst_ref=own_all.at[o2], send_sem=ssem_o.at[0, d],
                recv_sem=rsem_o.at[0, o2], device_id=peer, device_id_type=MESH),
            pltpu.make_async_remote_copy(
                src_ref=mix.at[0], dst_ref=mix_all.at[o2], send_sem=ssem_o.at[1, d],
                recv_sem=rsem_o.at[1, o2], device_id=peer, device_id_type=MESH),
        ]

    for d in range(1, no):
        for copy in small(d, o):
            copy.start()

    def prepare():
        for d in range(1, no):
            for copy in small(d, (o + d) % no):
                copy.wait_recv()
        for copy in local:
            copy.wait()
        table = pltpu.make_async_copy(own_all, own_tab, lsem.at[2])
        table.start()
        table.wait()

        def scan_source(s, carry):
            nxt[s, td] = td

            def back(n, following):
                t = td - 1 - n
                following = jnp.where(own_tab[s, 0, t] == o, t, following)
                nxt[s, t] = following
                return following

            lax.fori_loop(0, td, back, jnp.int32(td))
            return carry

        lax.fori_loop(0, no, scan_source, 0)

    gath[v] = amps[...]
    lanes = occ.shape[1]
    for r in range(occ.shape[0]):
        row = jnp.broadcast_to(occ[...].astype(jnp.float32)[r:r + 1], (128, lanes))
        occ_col[r * lanes:(r + 1) * lanes, :] = jnp.transpose(row)

    def tile_piece(o2, i, send_sem, device):
        window = pl.ds(i * chunk_tiles, chunk_tiles)
        return pltpu.make_async_remote_copy(
            src_ref=tiles.at[o2, window], dst_ref=tiles.at[o2, window], send_sem=send_sem,
            recv_sem=rsem_t.at[o2, i], device_id=device, device_id_type=MESH,
        )

    def group_of(d):
        return ((g + d) % ng) * 2

    def hand_on(i):
        for d in range(1, ng):
            o2 = group_of(d) + c
            tile_piece(o2, i, ssem_c.at[d], partner).wait_recv()
            tile_piece(o2, i, ssem_c.at[d], partner).start()

    def compute(i):
        first = pl.multiple_of(i * cr, cr)
        total = jnp.zeros((cr, cols), jnp.float32)
        for slot in range(nv):
            block = gath[slot, pl.ds(first, cr), :]
            column = slot * kw + lax.broadcasted_iota(jnp.int32, (1, kw), 1)
            low, high = slot * kw // k_tile, ((slot + 1) * kw - 1) // k_tile
            parts = []
            for n in range(chunk_tiles):
                t = i * chunk_tiles + n
                flag = jnp.full((1, kw), amp_mask[low, t].astype(jnp.float32))
                for s in range(low + 1, high + 1):
                    flag = jnp.where(column >= s * k_tile, amp_mask[s, t].astype(jnp.float32), flag)
                flag = jnp.broadcast_to(flag, (tr, kw)).astype(jnp.bfloat16)
                parts.append(block[n * tr:(n + 1) * tr] * flag)
            total += jnp.dot(
                jnp.concatenate(parts, axis=0), ints_v[slot * kw:(slot + 1) * kw, :],
                preferred_element_type=jnp.float32,
            )
        ladder = total.astype(jnp.bfloat16)
        for n in range(chunk_tiles):
            t = i * chunk_tiles + n
            kept = ladder[n * tr:(n + 1) * tr] * keep[0, t].astype(jnp.float32).astype(jnp.bfloat16)
            mixed = jnp.dot(mix_all[own_s[0, t]], kept, preferred_element_type=jnp.float32)
            energy = occ_col[pl.ds(pl.multiple_of(t * tr, tr), tr), :]
            denominator = vir[...] - jnp.concatenate([energy] * (cols // 128), axis=1)
            tiles[o, t] = (mixed / denominator).astype(jnp.bfloat16)

    def within(i, body):
        @pl.when((i >= 0) & (i < nc))
        def _():
            body(i)

    def send_own(i):
        spread(amps, v, i, True, True, False)

    def send_side(i):
        spread(amps, v, i, False, False, True)

    def turn(i):
        @pl.when(side_first(i))
        def _():
            slot = z * 2 + (1 - y)
            arrive(slot, i)
            spread(gath.at[slot], slot, i, True, True, False)

    def forward(j, i):
        for step_z, up in ((-j, True), (j, False)):
            near = z + step_z

            @pl.when((near >= 0) & (near < nz))
            def _():
                slot = near * 2 + y
                other = near * 2 + (1 - y)
                arrive(slot, i)
                spread(gath.at[slot], slot, i, up, not up, False)

                @pl.when(side_first(i))
                def _():
                    arrive(other, i)
                    spread(gath.at[other], other, i, up, not up, False)

                @pl.when(jnp.logical_not(side_first(i)))
                def _():
                    spread(gath.at[slot], slot, i, False, False, True)

    def finish(i):
        @pl.when(i == 0)
        def _():
            prepare()

        @pl.when(jnp.logical_not(side_first(i)))
        def _():
            for zz in range(nz):
                arrive(zz * 2 + (1 - y), i)

        compute(i)
        for d in range(1, ng):
            tile_piece(o, i, ssem_t.at[d], {"occ": group_of(d) + c, "vir": v}).start()
        tile_piece(o, i, ssem_c.at[0], partner).start()

    def step(s, carry):
        within(s + ahead, send_own)
        within(s + ahead_side, send_side)
        within(s, turn)
        for j in range(1, nz):
            within(s - stagger * j, functools.partial(forward, j))
        within(s - lag, finish)
        within(s - lag - 1, hand_on)
        return carry

    lax.fori_loop(0, nc + lag + 1, step, 0)

    def last(i, carry):
        for d in range(ng):
            tile_piece(group_of(d) + (1 - c), i, ssem_c.at[d], partner).wait_recv()
        return carry

    lax.fori_loop(0, nc, last, 0)

    def source(s, carry):
        def slot(k, position):
            t = nxt[s, position]
            tile = tiles[s, jnp.minimum(t, td - 1)]
            out[s * cap + k] = jnp.where(t < td, tile, jnp.zeros_like(tile))
            return jnp.minimum(t + 1, td)

        lax.fori_loop(0, cap, slot, jnp.int32(0))
        return carry

    lax.fori_loop(0, no, source, 0)

    def sent(whole, send_sem, recv_sem, device):
        pltpu.make_async_remote_copy(
            src_ref=whole, dst_ref=whole, send_sem=send_sem, recv_sem=recv_sem,
            device_id=device, device_id_type=MESH).wait_send()

    turned = sum(1 for i in range(nc) if side_first(i)) * cr
    full = gath.shape[1]
    for zz in range(nz):
        for slot, count in ((zz * 2 + y, full), (zz * 2 + (1 - y), turned)):
            if count:
                whole = gath.at[zz, pl.ds(0, count)]

                @pl.when((z < nz - 1) & (zz <= z))
                def _():
                    sent(whole, ssem_g.at[0, slot], rsem_g.at[0, 0], side)

                @pl.when((z > 0) & (zz >= z))
                def _():
                    sent(whole, ssem_g.at[1, slot], rsem_g.at[0, 0], side)

        @pl.when(zz == z)
        def _():
            sent(gath.at[zz], ssem_g.at[2, v], rsem_g.at[0, 0], side)

        if full > turned:
            @pl.when(zz != z)
            def _():
                part = gath.at[zz, pl.ds(0, full - turned)]
                sent(part, ssem_g.at[2, zz * 2 + y], rsem_g.at[0, 0], side)
    for d in range(ng):
        sent(tiles.at[d], ssem_c.at[d], rsem_t.at[0, 0], partner)
        if d:
            sent(tiles.at[d], ssem_t.at[d], rsem_t.at[0, 0], partner)
    for d in range(1, no):
        for copy in small(d, o):
            copy.wait_send()


def shards(no, nv, amps, ints, amp_mask, keep_mask, owners, occ_energy, vir_energy, mix):
    td, k_tiles = amp_mask.shape
    rows, kw = amps.shape
    tr = rows // td
    cols = ints.shape[1]
    k_tile = ints.shape[0] // k_tiles
    cap = max(2, 2 * td // no)
    chunk_tiles = max(1, min(td, 128 // tr))
    nc = td // chunk_tiles
    ahead, ahead_side, stagger, side_every = 2, 6, 1, 8
    lag = stagger * (nv // 2 - 1) + 1
    cfg = (no, nv, td, tr, chunk_tiles, k_tile, ahead, ahead_side, stagger, lag, side_every)
    smem = pl.BlockSpec(memory_space=pltpu.SMEM)
    vmem = pl.BlockSpec(memory_space=pltpu.VMEM)
    ng, nz = no // 2, nv // 2
    own = owners.reshape(1, td)
    return pl.pallas_call(
        functools.partial(ladder_kernel, cfg),
        out_shape=jax.ShapeDtypeStruct((no * cap, tr, cols), jnp.bfloat16),
        in_specs=[vmem, pl.BlockSpec(memory_space=pl.ANY), smem, smem, smem, vmem, vmem, vmem, vmem],
        out_specs=vmem,
        scratch_shapes=[
            pltpu.VMEM((nv, rows, kw), jnp.bfloat16),
            pltpu.VMEM(ints.shape, jnp.bfloat16),
            pltpu.VMEM((rows, 128), jnp.float32),
            pltpu.VMEM((no, td, tr, cols), jnp.bfloat16),
            pltpu.VMEM((no, tr, tr), jnp.bfloat16),
            pltpu.VMEM((no, 1, td), jnp.int32),
            pltpu.SMEM((no, 1, td), jnp.int32),
            pltpu.SMEM((no, td + 1), jnp.int32),
            pltpu.SemaphoreType.DMA((4,)),
            pltpu.SemaphoreType.DMA((nv, nc)),
            pltpu.SemaphoreType.DMA((3, nv)),
            pltpu.SemaphoreType.DMA((no, nc)),
            pltpu.SemaphoreType.DMA((ng,)),
            pltpu.SemaphoreType.DMA((ng,)),
            pltpu.SemaphoreType.DMA((2, no)),
            pltpu.SemaphoreType.DMA((2, no)),
        ],
        compiler_params=pltpu.CompilerParams(
            collective_id=0, has_side_effects=True, vmem_limit_bytes=60 * 1024 * 1024
        ),
    )(
        amps, ints, amp_mask.T, keep_mask.reshape(1, td), own, own,
        occ_energy.reshape(rows // 128, 128),
        vir_energy.reshape(1, cols), mix,
    )


def solution(mesh):
    in_specs = (
        P("occ", "vir"),
        P(None, "vir"),
        P("occ", None),
        P("occ", "vir"),
        P("occ", None),
        P("occ"),
        P("vir"),
        P("occ", None, None),
    )
    body = functools.partial(shards, mesh.shape["occ"], mesh.shape["vir"])
    return jax.shard_map(
        body, mesh=mesh, in_specs=in_specs, out_specs=P("occ", None, "vir"), check_vma=False
    )
```

profile of v0, /device:TPU:0, one launch (start us, length us, event | category | flops | bytes accessed | tf_op | source)
XLA Modules:
  0.0 81.5 jit_solution(16683141356703357548)
XLA Ops:
  0.0 78.3 %shard_map.82 = bf16[64,32,512]{2,1,0:T(8,128)(2,1)} custom-call(bf16[1024,384]{1,0:T(8,128)(2,1)} %amps.1, bf16[3072,512]{1,0:T(8,128)(2,1)} %ints.1, s32[6,32]{1,0:T(8,128)} %bitcast.5, s32[1,32]{1,0:T(1,128)} %bitcast.10, s32[1,32]{1,0:T(1,128)} %bitcast.8, s32[1,32]{1,0:T(1,128)} %bitcast.9, bf16[8,128]{1,0:T(8,128)(2,1)} %bitcast.6, f32[1,512]{1,0:T(1,128)} %bitcast.7, ...), custom_call_target="tpu_custom_call" | custom-call | tf_op jit(solution)/shard_map/pallas_call | solution.py:318
  78.3 3.2 %copy.10 = bf16[64,32,512]{2,1,0:T(8,128)(2,1)} copy(bf16[64,32,512]{2,1,0:T(8,128)(2,1)} %shard_map.82) | data formatting | bytes 4194304
where the time goes:
time: 82.4 us; the launch traced here: 81.5 us
  Pallas kernels  78.3 us (95%)
  local copies, waits for them, and re-layouts  3.16 us (4%)
    pallas_call x1, Pallas kernels, shards(): pl.pallas_call(functools.partial(ladder_kernel, cfg), out_shape=jax.Shape...  78.3 us
    unnamed x1, local copies, waits for them, and re-layouts  3.16 us

commit v1 on v0

v1 whole, which is shorter than its diff:
```python
import functools

import jax
import jax.numpy as jnp
from jax import lax
from jax.experimental import pallas as pl
from jax.experimental.pallas import tpu as pltpu
from jax.sharding import PartitionSpec as P

MESH = pl.DeviceIdType.MESH


def ladder_kernel(
    cfg, amps, ints, amp_mask, keep, own_s, own_v, occ, vir, mix, keep_v, out,
    gath, ints_own, ints_end, masked, occ_col, tiles, tiles_end, mix_all, own_all, own_tab, nxt,
    vir_end, keep_land, keep_end,
    lsem, rsem_g, ssem_g, rsem_b, ssem_b, ssem_bx, ssem_bc, rsem_t, ssem_c, ssem_t, ssem_r,
    rsem_o, ssem_o, rsem_s, ssem_s,
):
    no, nv, td, tr, chunk_tiles, k_tile, ahead, lead, nb = cfg
    ng, nz = no // 2, nv // 2
    rows, kw = amps.shape
    depth, cols = ints.shape
    cr = chunk_tiles * tr
    nc = rows // cr
    cap = out.shape[0] // no
    share = depth // no
    part = share // nb
    o, v = lax.axis_index("occ"), lax.axis_index("vir")
    g, c = o // 2, o % 2
    z, y = v // 2, v % 2
    mate = z * 2 + (1 - y)
    is_end = (z == 0) | (z == nz - 1)
    inner = jnp.logical_not(is_end)
    has_end = (z == 1) | (z == nz - 2)
    go_up = (z >= 1) & (z < nz - 2)
    go_down = (z > 1) & (z <= nz - 2)
    partner = {"occ": g * 2 + (1 - c), "vir": v}
    side = {"occ": o, "vir": mate}
    above = {"occ": o, "vir": (z + 1) * 2 + y}
    below = {"occ": o, "vir": (z - 1) * 2 + y}
    inward = {"occ": o, "vir": jnp.where(z == 0, 1, nz - 2) * 2 + y}
    outward = {"occ": o, "vir": jnp.where(z == 1, 0, nz - 1) * 2 + y}

    load_own = pltpu.make_async_copy(own_v, own_all.at[o], lsem.at[0])
    load_mix = pltpu.make_async_copy(mix.at[0], mix_all.at[o], lsem.at[1])
    load_ints = pltpu.make_async_copy(ints, ints_own, lsem.at[2])
    load_amps = pltpu.make_async_copy(amps, gath.at[v], lsem.at[3])
    load_own.start()
    load_mix.start()

    @pl.when(inner)
    def _():
        load_amps.start()
        load_ints.start()

    barrier = pltpu.get_barrier_semaphore()

    def greet(device):
        pl.semaphore_signal(barrier, inc=1, device_id=device, device_id_type=MESH)

    for d in range(1, no):
        greet({"occ": (o + d) % no, "vir": v})
    greet(side)

    @pl.when(z < nz - 1)
    def _():
        greet(above)

    @pl.when(z > 0)
    def _():
        greet(below)

    both = jnp.where(z < nz - 1, 1, 0) + jnp.where(z > 0, 1, 0)
    pl.semaphore_wait(barrier, no + both)

    def crosses_early(i):
        return (i % 3 != 0) | (i == nc - 1)

    early = sum(1 for i in range(nc) if i % 3 != 0 or i == nc - 1) * cr

    def piece(src, slot, i, send_sem, device):
        window = pl.ds(pl.multiple_of(i * cr, cr), cr)
        return pltpu.make_async_remote_copy(
            src_ref=src.at[window], dst_ref=gath.at[slot, window], send_sem=send_sem,
            recv_sem=rsem_g.at[slot, i], device_id=device, device_id_type=MESH,
        )

    def arrive(slot, i):
        piece(gath.at[slot], slot, i, ssem_g.at[2, 0], side).wait_recv()

    def small(d, o2):
        peer = {"occ": (o + d) % no, "vir": v}
        return [
            pltpu.make_async_remote_copy(
                src_ref=own_v, dst_ref=own_all.at[o2], send_sem=ssem_o.at[0, d],
                recv_sem=rsem_o.at[0, o2], device_id=peer, device_id_type=MESH),
            pltpu.make_async_remote_copy(
                src_ref=mix.at[0], dst_ref=mix_all.at[o2], send_sem=ssem_o.at[1, d],
                recv_sem=rsem_o.at[1, o2], device_id=peer, device_id_type=MESH),
        ]

    def end_rows():
        return [
            pltpu.make_async_remote_copy(
                src_ref=vir, dst_ref=vir_end, send_sem=ssem_s.at[0], recv_sem=rsem_s.at[0],
                device_id=inward, device_id_type=MESH),
            pltpu.make_async_remote_copy(
                src_ref=keep_v, dst_ref=keep_land, send_sem=ssem_s.at[1], recv_sem=rsem_s.at[1],
                device_id=inward, device_id_type=MESH),
        ]

    def table():
        for d in range(1, no):
            for copy in small(d, (o + d) % no):
                copy.wait_recv()
        load_own.wait()
        load_mix.wait()
        copy = pltpu.make_async_copy(own_all, own_tab, lsem.at[4])
        copy.start()
        copy.wait()

        def scan_source(s, carry):
            nxt[s, td] = td

            def back(n, following):
                t = td - 1 - n
                following = jnp.where(own_tab[s, 0, t] == o, t, following)
                nxt[s, t] = following
                return following

            lax.fori_loop(0, td, back, jnp.int32(td))
            return carry

        lax.fori_loop(0, no, scan_source, 0)

    def group_of(d):
        return ((g + d) % ng) * 2

    def tile_piece(o2, i, send_sem, device):
        window = pl.ds(i * chunk_tiles, chunk_tiles)
        return pltpu.make_async_remote_copy(
            src_ref=tiles.at[o2, window], dst_ref=tiles.at[o2, window], send_sem=send_sem,
            recv_sem=rsem_t.at[o2, i], device_id=device, device_id_type=MESH,
        )

    def back_piece(i):
        window = pl.ds(i * chunk_tiles, chunk_tiles)
        return pltpu.make_async_remote_copy(
            src_ref=tiles_end.at[window], dst_ref=tiles.at[o, window], send_sem=ssem_r.at[0],
            recv_sem=rsem_t.at[o, i], device_id=outward, device_id_type=MESH,
        )

    def share_out(i):
        for d in range(1, ng):
            tile_piece(o, i, ssem_t.at[d], {"occ": group_of(d) + c, "vir": v}).start()
        tile_piece(o, i, ssem_c.at[0], partner).start()

    def hand_on(i):
        for d in range(1, ng):
            o2 = group_of(d) + c
            tile_piece(o2, i, ssem_c.at[d], partner).wait_recv()
            tile_piece(o2, i, ssem_c.at[d], partner).start()

    def block(q, p):
        return pl.ds(pl.multiple_of(q * share + p * part, part), part)

    def ints_piece(src, q, p, send_sem, device):
        return pltpu.make_async_remote_copy(
            src_ref=src.at[block(q, p)], dst_ref=ints_end.at[block(q, p)], send_sem=send_sem,
            recv_sem=rsem_b.at[q, p], device_id=device, device_id_type=MESH,
        )

    def ints_arrive(q, p):
        ints_piece(ints_end, q, p, ssem_b.at[0], partner).wait_recv()

    @pl.when(is_end)
    def _():
        for copy in end_rows():
            copy.start()

        def cross(i, carry):
            @pl.when(crosses_early(i))
            def _():
                piece(amps, v, i, ssem_g.at[2, v], side).start()

            return carry

        lax.fori_loop(0, nc, cross, 0)

        def send_ints(p):
            ints_piece(ints, o, p, ssem_b.at[0], inward).start()

        def send_amps(i):
            piece(amps, v, i, ssem_g.at[0, v], inward).start()

            @pl.when(crosses_early(i))
            def _():
                arrive(mate, i)
                piece(gath.at[mate], mate, i, ssem_g.at[0, mate], inward).start()

        for p in range(nb - 1):
            send_ints(p)
        for d in range(1, no):
            for copy in small(d, o):
                copy.start()
        send_amps(0)
        send_ints(nb - 1)

        def rest(i, carry):
            send_amps(i)
            return carry

        lax.fori_loop(1, nc, rest, 0)
        table()

        def pass_on(i, carry):
            tile_piece(o, i, ssem_c.at[0], partner).wait_recv()
            share_out(i)

            @pl.when(i > 0)
            def _():
                hand_on(i - 1)

            return carry

        lax.fori_loop(0, nc, pass_on, 0)
        hand_on(nc - 1)

    def mask_rows(i):
        first = pl.multiple_of(i * cr, cr)
        for slot in range(nv):
            rows_in = gath[slot, pl.ds(first, cr), :]
            column = slot * kw + lax.broadcasted_iota(jnp.int32, (1, kw), 1)
            low, high = slot * kw // k_tile, ((slot + 1) * kw - 1) // k_tile
            for n in range(chunk_tiles):
                t = i * chunk_tiles + n
                flag = jnp.full((1, kw), amp_mask[low, t].astype(jnp.float32))
                for s in range(low + 1, high + 1):
                    flag = jnp.where(column >= s * k_tile, amp_mask[s, t].astype(jnp.float32), flag)
                flag = jnp.broadcast_to(flag, (tr, kw)).astype(jnp.bfloat16)
                masked[slot, n * tr:(n + 1) * tr, :] = rows_in[n * tr:(n + 1) * tr] * flag

    def ladder_of(right):
        if kw % 128 == 0:
            left = jnp.concatenate([masked[slot] for slot in range(nv)], axis=1)
            return jnp.dot(left, right[...], preferred_element_type=jnp.float32)
        total = jnp.zeros((cr, cols), jnp.float32)
        for slot in range(nv):
            total += jnp.dot(
                masked[slot], right[slot * kw:(slot + 1) * kw, :], preferred_element_type=jnp.float32)
        return total

    def update(i, right, keep_row, vir_row, store):
        ladder = ladder_of(right).astype(jnp.bfloat16)
        for n in range(chunk_tiles):
            t = i * chunk_tiles + n
            kept = ladder[n * tr:(n + 1) * tr] * keep_row[0, t].astype(jnp.float32).astype(jnp.bfloat16)
            mixed = jnp.dot(mix_all[own_s[0, t]], kept, preferred_element_type=jnp.float32)
            energy = occ_col[pl.ds(pl.multiple_of(t * tr, tr), tr), :]
            denominator = vir_row[...] - jnp.concatenate([energy] * (cols // 128), axis=1)
            store(t, (mixed / denominator).astype(jnp.bfloat16))

    @pl.when(inner)
    def _():
        def send_own(i):
            @pl.when(go_up)
            def _():
                piece(amps, v, i, ssem_g.at[0, v], above).start()

            @pl.when(go_down)
            def _():
                piece(amps, v, i, ssem_g.at[1, v], below).start()

        def send_side(i):
            piece(amps, v, i, ssem_g.at[2, v], side).start()

        for i in range(min(ahead, nc)):
            send_side(i)

        def all_own(i, carry):
            send_own(i)
            return carry

        lax.fori_loop(0, nc, all_own, 0)
        for d in range(1, no):
            for copy in small(d, o):
                copy.start()

        lanes = occ.shape[1]
        for r in range(occ.shape[0]):
            row = jnp.broadcast_to(occ[...].astype(jnp.float32)[r:r + 1], (128, lanes))
            occ_col[r * lanes:(r + 1) * lanes, :] = jnp.transpose(row)

        def within(i, body):
            @pl.when((i >= 0) & (i < nc))
            def _():
                body(i)

        def relay(slot, i, up):
            ok, sem, device = (go_up, 0, above) if up else (go_down, 1, below)

            @pl.when(ok)
            def _():
                piece(gath.at[slot], slot, i, ssem_g.at[sem, slot], device).start()

        def from_inner(j, i):
            for near, up in ((z - j, True), (z + j, False)):
                @pl.when((near >= 1) & (near <= nz - 2))
                def _():
                    slot = near * 2 + y
                    arrive(slot, i)
                    relay(slot, i, up)
                    piece(gath.at[slot], slot, i, ssem_g.at[2, slot], side).start()

        def from_end(j, i):
            for near, end, up in ((z - j, 0, True), (z + j, nz - 1, False)):
                @pl.when(near == end)
                def _():
                    slot = end * 2 + y
                    other = end * 2 + (1 - y)
                    arrive(slot, i)
                    relay(slot, i, up)

                    @pl.when(crosses_early(i))
                    def _():
                        arrive(other, i)
                        relay(other, i, up)

                    @pl.when(jnp.logical_not(crosses_early(i)))
                    def _():
                        piece(gath.at[slot], slot, i, ssem_g.at[2, slot], side).start()

        def from_outward(p):
            @pl.when(has_end)
            def _():
                ints_arrive(o, p)
                for d in range(1, ng):
                    ints_piece(ints_end, o, p, ssem_bx.at[d], {"occ": group_of(d) + c, "vir": v}).start()
                ints_piece(ints_end, o, p, ssem_bc.at[0], partner).start()

        def ints_on(p):
            @pl.when(has_end)
            def _():
                for d in range(1, ng):
                    ints_arrive(group_of(d) + c, p)
                    ints_piece(ints_end, group_of(d) + c, p, ssem_bc.at[d], partner).start()

        def ints_last():
            for p in range(nb):
                for d in range(ng):
                    ints_arrive(group_of(d) + (1 - c), p)
            for copy in end_rows():
                copy.wait_recv()
            copy = pltpu.make_async_copy(keep_land, keep_end, lsem.at[5])
            copy.start()
            copy.wait()

        def finish(i):
            for zz in range(1, nz - 1):
                arrive(zz * 2 + (1 - y), i)

            @pl.when(jnp.logical_not(crosses_early(i)))
            def _():
                arrive(1 - y, i)
                arrive((nz - 1) * 2 + (1 - y), i)

            @pl.when(i == 0)
            def _():
                load_ints.wait()
                load_amps.wait()
                table()

            mask_rows(i)

            @pl.when(has_end)
            def _():
                @pl.when(i == 0)
                def _():
                    ints_last()

                def store_end(t, value):
                    tiles_end[t] = value

                update(i, ints_end, keep_end, vir_end, store_end)
                back_piece(i).start()

            def store_own(t, value):
                tiles[o, t] = value

            update(i, ints_own, keep, vir, store_own)
            share_out(i)

        lag = nz - 3

        def step(s, carry):
            if nz == 4:
                n = jnp.where(s < 5, s, jnp.where(s % 2 == 0, 2 + s // 2, nc + nz))
            else:
                n = s
            within(n + ahead, send_side)
            for j in range(1, nz - 2):
                within(n - (j - 1), functools.partial(from_inner, j))

            @pl.when(s < nb - 1)
            def _():
                from_outward(s)

            @pl.when(s == nb)
            def _():
                from_outward(nb - 1)

            @pl.when((s >= 1) & (s < nb))
            def _():
                ints_on(s - 1)

            e = s - lead
            for j in range(1, nz - 1):
                within(e - (j - 1), functools.partial(from_end, j))

            @pl.when(s == nb)
            def _():
                ints_on(nb - 1)

            within(e - lag, finish)
            within(e - lag - 1, hand_on)
            return carry

        lax.fori_loop(0, nc + lead + lag + 1, step, 0)

    def last(i, carry):
        for d in range(ng):
            tile_piece(group_of(d) + (1 - c), i, ssem_c.at[d], partner).wait_recv()
        return carry

    lax.fori_loop(0, nc, last, 0)

    def source(s, carry):
        def slot(k, position):
            t = nxt[s, position]
            tile = tiles[s, jnp.minimum(t, td - 1)]
            out[s * cap + k] = jnp.where(t < td, tile, jnp.zeros_like(tile))
            return jnp.minimum(t + 1, td)

        lax.fori_loop(0, cap, slot, jnp.int32(0))
        return carry

    lax.fori_loop(0, no, source, 0)

    def sent(whole, send_sem, recv_sem):
        pltpu.make_async_remote_copy(
            src_ref=whole, dst_ref=whole, send_sem=send_sem, recv_sem=recv_sem,
            device_id=partner, device_id_type=MESH).wait_send()

    def sent_rows(count, direction, slot):
        if count:
            sent(gath.at[0, pl.ds(0, count)], ssem_g.at[direction, slot], rsem_g.at[0, 0])

    @pl.when(is_end)
    def _():
        sent_rows(early, 2, v)
        sent_rows(rows, 0, v)
        sent_rows(early, 0, mate)
        sent(ints_end.at[pl.ds(0, share)], ssem_b.at[0], rsem_b.at[0, 0])
        for copy in end_rows():
            copy.wait_send()

    @pl.when(inner)
    def _():
        sent_rows(rows, 2, v)
        for zz in range(nz):
            is_far = zz in (0, nz - 1)
            for direction, ok, along in ((0, go_up, zz <= z), (1, go_down, zz >= z)):
                @pl.when(ok & along)
                def _():
                    sent_rows(rows, direction, zz * 2 + y)
                    if is_far:
                        sent_rows(early, direction, zz * 2 + (1 - y))

            @pl.when(zz != z)
            def _():
                sent_rows(rows - early if is_far else rows, 2, zz * 2 + y)

        @pl.when(has_end)
        def _():
            for d in range(ng):
                whole = ints_end.at[pl.ds(0, share)]
                sent(whole, ssem_bc.at[d], rsem_b.at[0, 0])
                if d:
                    sent(whole, ssem_bx.at[d], rsem_b.at[0, 0])
            sent(tiles_end, ssem_r.at[0], rsem_t.at[0, 0])

    for d in range(ng):
        sent(tiles.at[d], ssem_c.at[d], rsem_t.at[0, 0])
        if d:
            sent(tiles.at[d], ssem_t.at[d], rsem_t.at[0, 0])
    for d in range(1, no):
        for copy in small(d, o):
            copy.wait_send()


def shards(no, nv, amps, ints, amp_mask, keep_mask, owners, occ_energy, vir_energy, mix):
    td, k_tiles = amp_mask.shape
    rows, kw = amps.shape
    tr = rows // td
    cols = ints.shape[1]
    k_tile = ints.shape[0] // k_tiles
    cap = max(2, 2 * td // no)
    chunk_tiles = max(1, min(td, 128 // tr))
    nc = td // chunk_tiles
    ahead, lead, nb = 2, 3, 4
    cfg = (no, nv, td, tr, chunk_tiles, k_tile, ahead, lead, nb)
    smem = pl.BlockSpec(memory_space=pltpu.SMEM)
    vmem = pl.BlockSpec(memory_space=pltpu.VMEM)
    hbm = pl.BlockSpec(memory_space=pl.ANY)
    ng = no // 2
    own = owners.reshape(1, td)
    keep = keep_mask.reshape(1, td)
    dma = pltpu.SemaphoreType.DMA
    return pl.pallas_call(
        functools.partial(ladder_kernel, cfg),
        out_shape=jax.ShapeDtypeStruct((no * cap, tr, cols), jnp.bfloat16),
        in_specs=[hbm, hbm, smem, smem, smem, vmem, vmem, vmem, vmem, vmem],
        out_specs=vmem,
        scratch_shapes=[
            pltpu.VMEM((nv, rows, kw), jnp.bfloat16),
            pltpu.VMEM(ints.shape, jnp.bfloat16),
            pltpu.VMEM(ints.shape, jnp.bfloat16),
            pltpu.VMEM((nv, chunk_tiles * tr, kw), jnp.bfloat16),
            pltpu.VMEM((rows, 128), jnp.float32),
            pltpu.VMEM((no, td, tr, cols), jnp.bfloat16),
            pltpu.VMEM((td, tr, cols), jnp.bfloat16),
            pltpu.VMEM((no, tr, tr), jnp.bfloat16),
            pltpu.VMEM((no, 1, td), jnp.int32),
            pltpu.SMEM((no, 1, td), jnp.int32),
            pltpu.SMEM((no, td + 1), jnp.int32),
            pltpu.VMEM((1, cols), jnp.float32),
            pltpu.VMEM((1, td), jnp.int32),
            pltpu.SMEM((1, td), jnp.int32),
            dma((6,)),
            dma((nv, nc)),
            dma((3, nv)),
            dma((no, nb)),
            dma((1,)),
            dma((ng,)),
            dma((ng,)),
            dma((no, nc)),
            dma((ng,)),
            dma((ng,)),
            dma((1,)),
            dma((2, no)),
            dma((2, no)),
            dma((2,)),
            dma((2,)),
        ],
        compiler_params=pltpu.CompilerParams(
            collective_id=0, has_side_effects=True, vmem_limit_bytes=60 * 1024 * 1024
        ),
    )(
        amps, ints, amp_mask.T, keep, own, own,
        occ_energy.reshape(rows // 128, 128),
        vir_energy.reshape(1, cols), mix, keep,
    )


def solution(mesh):
    in_specs = (
        P("occ", "vir"),
        P(None, "vir"),
        P("occ", None),
        P("occ", "vir"),
        P("occ", None),
        P("occ"),
        P("vir"),
        P("occ", None, None),
    )
    body = functools.partial(shards, mesh.shape["occ"], mesh.shape["vir"])
    return jax.shard_map(
        body, mesh=mesh, in_specs=in_specs, out_specs=P("occ", None, "vir"), check_vma=False
    )
```

time: 82.4 us -> 87.8 us (1.066)
  Pallas kernels: 78.3 us -> 83.7 us
    pallas_call x1, Pallas kernels: 78.3 us -> 83.7 us  [shards(): pl.pallas_call(functools.partial(ladder_kernel, cfg), out_shape=jax.Shape...]
where the time goes in v1:
time: 87.8 us; the launch traced here: 86.9 us
  Pallas kernels  83.7 us (95%)
  local copies, waits for them, and re-layouts  3.16 us (4%)
    pallas_call x1, Pallas kernels, shards(): pl.pallas_call(functools.partial(ladder_kernel, cfg), out_shape=jax.Shape...  83.7 us
    unnamed x1, local copies, waits for them, and re-layouts  3.16 us

profile of v1, /device:TPU:0, one launch (start us, length us, event | category | flops | bytes accessed | tf_op | source)
XLA Modules:
  0.0 86.9 jit_solution(14862460058428505463)
XLA Ops:
  0.0 83.7 %shard_map.82 = bf16[64,32,512]{2,1,0:T(8,128)(2,1)} custom-call(bf16[1024,384]{1,0:T(8,128)(2,1)} %amps.1, bf16[3072,512]{1,0:T(8,128)(2,1)} %ints.1, s32[6,32]{1,0:T(8,128)} %bitcast.5, s32[1,32]{1,0:T(1,128)} %bitcast.8, s32[1,32]{1,0:T(1,128)} %bitcast.10, s32[1,32]{1,0:T(1,128)} %bitcast.11, bf16[8,128]{1,0:T(8,128)(2,1)} %bitcast.6, f32[1,512]{1,0:T(1,128)} %bitcast.7, ...), custom_call_target="tpu_custom_call" | custom-call | tf_op jit(solution)/shard_map/pallas_call | solution.py:520
  83.7 3.2 %copy.10 = bf16[64,32,512]{2,1,0:T(8,128)(2,1)} copy(bf16[64,32,512]{2,1,0:T(8,128)(2,1)} %shard_map.82) | data formatting | bytes 4194304

commit v2 on v1

--- a/solution.py
+++ b/solution.py
@@ -17,12 +17,15 @@
     lsem, rsem_g, ssem_g, rsem_b, ssem_b, ssem_bx, ssem_bc, rsem_t, ssem_c, ssem_t, ssem_r,
     rsem_o, ssem_o, rsem_s, ssem_s,
 ):
-    no, nv, td, tr, chunk_tiles, k_tile, ahead, lead, nb = cfg
+    no, nv, td, tr, chunk_tiles, k_tile, ahead, lead, nb, late = cfg
     ng, nz = no // 2, nv // 2
     rows, kw = amps.shape
     depth, cols = ints.shape
     cr = chunk_tiles * tr
     nc = rows // cr
+    pt = chunk_tiles // 2
+    pr = pt * tr
+    np_ = rows // pr
     cap = out.shape[0] // no
     share = depth // no
     part = share // nb
@@ -75,12 +78,12 @@
     pl.semaphore_wait(barrier, no + both)
 
     def crosses_early(i):
-        return (i % 3 != 0) | (i == nc - 1)
-
-    early = sum(1 for i in range(nc) if i % 3 != 0 or i == nc - 1) * cr
+        return (i % 3 != 1) | (i >= late)
+
+    early = sum(1 for i in range(np_) if i % 3 != 1 or i >= late) * pr
 
     def piece(src, slot, i, send_sem, device):
-        window = pl.ds(pl.multiple_of(i * cr, cr), cr)
+        window = pl.ds(pl.multiple_of(i * pr, pr), pr)
         return pltpu.make_async_remote_copy(
             src_ref=src.at[window], dst_ref=gath.at[slot, window], send_sem=send_sem,
             recv_sem=rsem_g.at[slot, i], device_id=device, device_id_type=MESH,
@@ -138,14 +141,14 @@
         return ((g + d) % ng) * 2
 
     def tile_piece(o2, i, send_sem, device):
-        window = pl.ds(i * chunk_tiles, chunk_tiles)
+        window = pl.ds(i * pt, pt)
         return pltpu.make_async_remote_copy(
             src_ref=tiles.at[o2, window], dst_ref=tiles.at[o2, window], send_sem=send_sem,
             recv_sem=rsem_t.at[o2, i], device_id=device, device_id_type=MESH,
         )
 
     def back_piece(i):
-        window = pl.ds(i * chunk_tiles, chunk_tiles)
+        window = pl.ds(i * pt, pt)
         return pltpu.make_async_remote_copy(
             src_ref=tiles_end.at[window], dst_ref=tiles.at[o, window], send_sem=ssem_r.at[0],
             recv_sem=rsem_t.at[o, i], device_id=outward, device_id_type=MESH,
@@ -186,7 +189,7 @@
 
             return carry
 
-        lax.fori_loop(0, nc, cross, 0)
+        lax.fori_loop(0, np_, cross, 0)
 
         def send_ints(p):
             ints_piece(ints, o, p, ssem_b.at[0], inward).start()
@@ -211,21 +214,22 @@
             send_amps(i)
             return carry
 
-        lax.fori_loop(1, nc, rest, 0)
+        lax.fori_loop(1, np_, rest, 0)
         table()
 
         def pass_on(i, carry):
             tile_piece(o, i, ssem_c.at[0], partner).wait_recv()
             share_out(i)
 
-            @pl.when(i > 0)
-            def _():
-                hand_on(i - 1)
+            @pl.when(i >= 3)
+            def _():
+                hand_on(i - 3)
 
             return carry
 
-        lax.fori_loop(0, nc, pass_on, 0)
-        hand_on(nc - 1)
+        lax.fori_loop(0, np_, pass_on, 0)
+        for i in range(np_ - 3, np_):
+            hand_on(i)
 
     def mask_rows(i):
         first = pl.multiple_of(i * cr, cr)
@@ -251,7 +255,7 @@
                 masked[slot], right[slot * kw:(slot + 1) * kw, :], preferred_element_type=jnp.float32)
         return total
 
-    def update(i, right, keep_row, vir_row, store):
+    def update(i, right, keep_row, vir_row, store, send):
         ladder = ladder_of(right).astype(jnp.bfloat16)
         for n in range(chunk_tiles):
             t = i * chunk_tiles + n
@@ -260,6 +264,8 @@
             energy = occ_col[pl.ds(pl.multiple_of(t * tr, tr), tr), :]
             denominator = vir_row[...] - jnp.concatenate([energy] * (cols // 128), axis=1)
             store(t, (mixed / denominator).astype(jnp.bfloat16))
+            if n % pt == pt - 1:
+                send(2 * i + n // pt)
 
     @pl.when(inner)
     def _():
@@ -275,14 +281,14 @@
         def send_side(i):
             piece(amps, v, i, ssem_g.at[2, v], side).start()
 
-        for i in range(min(ahead, nc)):
+        for i in range(min(ahead, np_)):
             send_side(i)
 
         def all_own(i, carry):
             send_own(i)
             return carry
 
-        lax.fori_loop(0, nc, all_own, 0)
+        lax.fori_loop(0, np_, all_own, 0)
         for d in range(1, no):
             for copy in small(d, o):
                 copy.start()
@@ -293,7 +299,7 @@
             occ_col[r * lanes:(r + 1) * lanes, :] = jnp.transpose(row)
 
         def within(i, body):
-            @pl.when((i >= 0) & (i < nc))
+            @pl.when((i >= 0) & (i < np_))
             def _():
                 body(i)
 
@@ -356,84 +362,144 @@
             copy.start()
             copy.wait()
 
-        def finish(i):
-            for zz in range(1, nz - 1):
-                arrive(zz * 2 + (1 - y), i)
-
-            @pl.when(jnp.logical_not(crosses_early(i)))
-            def _():
-                arrive(1 - y, i)
-                arrive((nz - 1) * 2 + (1 - y), i)
-
-            @pl.when(i == 0)
+        def compute_end(i):
+            for q in (2 * i, 2 * i + 1):
+                for zz in range(1, nz - 1):
+                    arrive(zz * 2 + (1 - y), q)
+
+                @pl.when(jnp.logical_not(crosses_early(q)))
+                def _():
+                    arrive(1 - y, q)
+                    arrive((nz - 1) * 2 + (1 - y), q)
+
+            mask_rows(i)
+
+            @pl.when(has_end)
+            def _():
+                @pl.when(i == 0)
+                def _():
+                    ints_last()
+
+                def store_end(t, value):
+                    tiles_end[t] = value
+
+                update(i, ints_end, keep_end, vir_end, store_end, lambda q: back_piece(q).start())
+
+        def compute_own(i):
+            def store_own(t, value):
+                tiles[o, t] = value
+
+            update(i, ints_own, keep, vir, store_own, share_out)
+
+            @pl.when(i >= 2)
+            def _():
+                hand_on(2 * i - 4)
+                hand_on(2 * i - 3)
+
+        b_in = {1: (0, 1), 3: (2, 3), 5: (4, 5, 6), 7: (7,)}
+        b_on = {3: (0, 1), 5: (2, 3), 6: (4, 5), 7: (6,), 9: (7,)}
+        lag = 2 * (nz - 3) + 2
+
+        def near_part(n):
+            within(n + ahead, send_side)
+            for j in range(1, nz - 2):
+                within(n - (j - 1), functools.partial(from_inner, j))
+
+        def parts_at(s, events, body):
+            for at, parts in events.items():
+                @pl.when(s == at)
+                def _():
+                    for p in parts:
+                        body(p)
+
+        def before(s):
+            parts_at(s, b_in, from_outward)
+
+            @pl.when(s == 2)
             def _():
                 load_ints.wait()
                 load_amps.wait()
                 table()
 
-            mask_rows(i)
-
-            @pl.when(has_end)
-            def _():
-                @pl.when(i == 0)
-                def _():
-                    ints_last()
-
-                def store_end(t, value):
-                    tiles_end[t] = value
-
-                update(i, ints_end, keep_end, vir_end, store_end)
-                back_piece(i).start()
-
-            def store_own(t, value):
-                tiles[o, t] = value
-
-            update(i, ints_own, keep, vir, store_own)
-            share_out(i)
-
-        lag = nz - 3
-
-        def step(s, carry):
-            if nz == 4:
-                n = jnp.where(s < 5, s, jnp.where(s % 2 == 0, 2 + s // 2, nc + nz))
-            else:
-                n = s
-            within(n + ahead, send_side)
-            for j in range(1, nz - 2):
-                within(n - (j - 1), functools.partial(from_inner, j))
-
-            @pl.when(s < nb - 1)
-            def _():
-                from_outward(s)
-
-            @pl.when(s == nb)
-            def _():
-                from_outward(nb - 1)
-
-            @pl.when((s >= 1) & (s < nb))
-            def _():
-                ints_on(s - 1)
-
-            e = s - lead
+        def far_part(e):
             for j in range(1, nz - 1):
-                within(e - (j - 1), functools.partial(from_end, j))
-
-            @pl.when(s == nb)
-            def _():
-                ints_on(nb - 1)
-
-            within(e - lag, finish)
-            within(e - lag - 1, hand_on)
-            return carry
-
-        lax.fori_loop(0, nc + lead + lag + 1, step, 0)
+                within(e - 2 * (j - 1), functools.partial(from_end, j))
+
+        def loop(low, high, body):
+            def one(i, carry):
+                body(i)
+                return carry
+
+            lax.fori_loop(low, high, one, 0)
+
+        if nz == 4:
+            def opening(s):
+                near_part(s)
+                before(s)
+                parts_at(s, b_on, ints_on)
+
+            def early_step(e):
+                near_part(lead + e - e // 4)
+                before(lead + e)
+                far_part(e)
+                parts_at(lead + e, b_on, ints_on)
+
+            def step(e):
+                @pl.when(e % 4 != 3)
+                def _():
+                    near_part(lead + e - e // 4)
+
+                far_part(e)
+
+            def pair(k):
+                step(2 * k + lag + 1)
+                compute_end(k)
+                step(2 * k + lag + 2)
+                compute_own(k)
+
+            def dense(k):
+                step(k + nc + lag - 3)
+                compute_end(k)
+                compute_own(k)
+
+            def closing(k):
+                step(2 * k + lag - 1)
+                compute_end(k)
+                step(2 * k + lag)
+                compute_own(k)
+
+            loop(0, lead, opening)
+            loop(0, 3, early_step)
+            loop(3, 4, lambda e: (before(lead + e), far_part(e), parts_at(lead + e, b_on, ints_on)))
+            loop(4, lag + 1, step)
+            loop(0, nc - 4, pair)
+            loop(nc - 4, nc - 2, dense)
+            loop(nc - 2, nc, closing)
+        else:
+            def step(s):
+                near_part(s)
+                before(s)
+                e = s - lead
+                far_part(e)
+                parts_at(s, b_on, ints_on)
+
+                @pl.when((e > lag) & ((e - lag) % 2 == 1) & (e < lag + 2 * nc))
+                def _():
+                    k = (e - lag - 1) // 2
+                    compute_end(k)
+                    compute_own(k)
+
+            loop(0, lead + np_ + lag, step)
+
+        for i in range(np_ - 4, np_):
+            hand_on(i)
 
     def last(i, carry):
         for d in range(ng):
             tile_piece(group_of(d) + (1 - c), i, ssem_c.at[d], partner).wait_recv()
         return carry
 
-    lax.fori_loop(0, nc, last, 0)
+    lax.fori_loop(0, np_, last, 0)
 
     def source(s, carry):
         def slot(k, position):
@@ -508,8 +574,9 @@
     cap = max(2, 2 * td // no)
     chunk_tiles = max(1, min(td, 128 // tr))
     nc = td // chunk_tiles
-    ahead, lead, nb = 2, 3, 4
-    cfg = (no, nv, td, tr, chunk_tiles, k_tile, ahead, lead, nb)
+    pieces = 2 * nc
+    ahead, lead, nb, late = 4, 6, 8, 3 * pieces // 4
+    cfg = (no, nv, td, tr, chunk_tiles, k_tile, ahead, lead, nb, late)
     smem = pl.BlockSpec(memory_space=pltpu.SMEM)
     vmem = pl.BlockSpec(memory_space=pltpu.VMEM)
     hbm = pl.BlockSpec(memory_space=pl.ANY)
@@ -538,13 +605,13 @@
             pltpu.VMEM((1, td), jnp.int32),
             pltpu.SMEM((1, td), jnp.int32),
             dma((6,)),
-            dma((nv, nc)),
+            dma((nv, pieces)),
             dma((3, nv)),
             dma((no, nb)),
             dma((1,)),
             dma((ng,)),
             dma((ng,)),
-            dma((no, nc)),
+            dma((no, pieces)),
             dma((ng,)),
             dma((ng,)),
             dma((1,)),

time: 87.8 us -> 76.6 us (0.87)
  Pallas kernels: 83.7 us -> 72.8 us
    pallas_call x1, Pallas kernels: 83.7 us -> 72.8 us  [shards(): pl.pallas_call(functools.partial(ladder_kernel, cfg), out_shape=jax.Shape...]
where the time goes in v2:
time: 76.6 us; the launch traced here: 75.9 us
  Pallas kernels  72.8 us (95%)
  local copies, waits for them, and re-layouts  3.16 us (4%)
    pallas_call x1, Pallas kernels, shards(): pl.pallas_call(functools.partial(ladder_kernel, cfg), out_shape=jax.Shape...  72.8 us
    unnamed x1, local copies, waits for them, and re-layouts  3.16 us

profile of v2, /device:TPU:0, one launch (start us, length us, event | category | flops | bytes accessed | tf_op | source)
XLA Modules:
  0.0 75.9 jit_solution(9043740884311119901)
XLA Ops:
  0.0 72.8 %shard_map.82 = bf16[64,32,512]{2,1,0:T(8,128)(2,1)} custom-call(bf16[1024,384]{1,0:T(8,128)(2,1)} %amps.1, bf16[3072,512]{1,0:T(8,128)(2,1)} %ints.1, s32[6,32]{1,0:T(8,128)} %bitcast.5, s32[1,32]{1,0:T(1,128)} %bitcast.8, s32[1,32]{1,0:T(1,128)} %bitcast.10, s32[1,32]{1,0:T(1,128)} %bitcast.11, bf16[8,128]{1,0:T(8,128)(2,1)} %bitcast.6, f32[1,512]{1,0:T(1,128)} %bitcast.7, ...), custom_call_target="tpu_custom_call" | custom-call | tf_op jit(solution)/shard_map/pallas_call | solution.py:587
  72.8 3.2 %copy.10 = bf16[64,32,512]{2,1,0:T(8,128)(2,1)} copy(bf16[64,32,512]{2,1,0:T(8,128)(2,1)} %shard_map.82) | data formatting | bytes 4194304

commit v3 on v2

--- a/solution.py
+++ b/solution.py
@@ -11,13 +11,13 @@
 
 
 def ladder_kernel(
-    cfg, amps, ints, amp_mask, keep, own_s, own_v, occ, vir, mix, keep_v, out,
-    gath, ints_own, ints_end, masked, occ_col, tiles, tiles_end, mix_all, own_all, own_tab, nxt,
+    cfg, amps, ints, amp_mask_in, keep_in, own_in, occ_in, vir_in, mix, tiles, order,
+    amp_mask, keep, own_s, occ, vir, gath, ints_own, ints_end, masked, occ_col, tiles_end, mix_all, own_all, own_tab, nxt,
     vir_end, keep_land, keep_end,
-    lsem, rsem_g, ssem_g, rsem_b, ssem_b, ssem_bx, ssem_bc, rsem_t, ssem_c, ssem_t, ssem_r,
+    lsem, rsem_n, rsem_e, ssem_g, rsem_b, ssem_b, ssem_bx, ssem_bc, rsem_t, ssem_c, ssem_t, ssem_r,
     rsem_o, ssem_o, rsem_s, ssem_s,
 ):
-    no, nv, td, tr, chunk_tiles, k_tile, ahead, lead, nb, late = cfg
+    no, nv, td, tr, chunk_tiles, k_tile, lead, nb, late = cfg
     ng, nz = no // 2, nv // 2
     rows, kw = amps.shape
     depth, cols = ints.shape
@@ -26,7 +26,6 @@
     pt = chunk_tiles // 2
     pr = pt * tr
     np_ = rows // pr
-    cap = out.shape[0] // no
     share = depth // no
     part = share // nb
     o, v = lax.axis_index("occ"), lax.axis_index("vir")
@@ -45,58 +44,75 @@
     inward = {"occ": o, "vir": jnp.where(z == 0, 1, nz - 2) * 2 + y}
     outward = {"occ": o, "vir": jnp.where(z == 1, 0, nz - 1) * 2 + y}
 
-    load_own = pltpu.make_async_copy(own_v, own_all.at[o], lsem.at[0])
+    barrier = pltpu.get_barrier_semaphore()
+
+    def greet(device):
+        pl.semaphore_signal(barrier, inc=1, device_id=device, device_id_type=MESH)
+
+    for d in range(1, no):
+        greet({"occ": (o + d) % no, "vir": v})
+    greet(side)
+
+    @pl.when(z < nz - 1)
+    def _():
+        greet(above)
+
+    @pl.when(z > 0)
+    def _():
+        greet(below)
+
+    load_own = pltpu.make_async_copy(own_in, own_all.at[o], lsem.at[0])
     load_mix = pltpu.make_async_copy(mix.at[0], mix_all.at[o], lsem.at[1])
     load_ints = pltpu.make_async_copy(ints, ints_own, lsem.at[2])
     load_amps = pltpu.make_async_copy(amps, gath.at[v], lsem.at[3])
+    loads = [
+        pltpu.make_async_copy(src, dst, lsem.at[7 + n])
+        for n, (src, dst) in enumerate(
+            ((amp_mask_in, amp_mask), (keep_in, keep), (own_in, own_s), (occ_in, occ), (vir_in, vir)))
+    ]
     load_own.start()
     load_mix.start()
 
     @pl.when(inner)
     def _():
+        for copy in loads:
+            copy.start()
         load_amps.start()
         load_ints.start()
 
-    barrier = pltpu.get_barrier_semaphore()
-
-    def greet(device):
-        pl.semaphore_signal(barrier, inc=1, device_id=device, device_id_type=MESH)
-
-    for d in range(1, no):
-        greet({"occ": (o + d) % no, "vir": v})
-    greet(side)
-
-    @pl.when(z < nz - 1)
-    def _():
-        greet(above)
-
-    @pl.when(z > 0)
-    def _():
-        greet(below)
-
     both = jnp.where(z < nz - 1, 1, 0) + jnp.where(z > 0, 1, 0)
     pl.semaphore_wait(barrier, no + both)
 
     def crosses_early(i):
-        return (i % 3 != 1) | (i >= late)
-
-    early = sum(1 for i in range(np_) if i % 3 != 1 or i >= late) * pr
-
-    def piece(src, slot, i, send_sem, device):
+        return (i < late) | (i >= late + np_ // 2) | (i % 2 == 1)
+
+    early = sum(1 for i in range(np_) if i < late or i >= late + np_ // 2 or i % 2 == 1) * pr
+
+    def piece(src, slot, far, i, send_sem, device):
         window = pl.ds(pl.multiple_of(i * pr, pr), pr)
         return pltpu.make_async_remote_copy(
             src_ref=src.at[window], dst_ref=gath.at[slot, window], send_sem=send_sem,
-            recv_sem=rsem_g.at[slot, i], device_id=device, device_id_type=MESH,
+            recv_sem=rsem_e.at[far, i], device_id=device, device_id_type=MESH,
         )
 
-    def arrive(slot, i):
-        piece(gath.at[slot], slot, i, ssem_g.at[2, 0], side).wait_recv()
+    def chunk(src, slot, i, send_sem, device):
+        window = pl.ds(pl.multiple_of(i * cr, cr), cr)
+        return pltpu.make_async_remote_copy(
+            src_ref=src.at[window], dst_ref=gath.at[slot, window], send_sem=send_sem,
+            recv_sem=rsem_n.at[slot - 2, i], device_id=device, device_id_type=MESH,
+        )
+
+    def arrive(slot, far, i):
+        piece(gath.at[slot], slot, far, i, ssem_g.at[2, 0], side).wait_recv()
+
+    def arrive_chunk(slot, i):
+        chunk(gath.at[slot], slot, i, ssem_g.at[2, 0], side).wait_recv()
 
     def small(d, o2):
         peer = {"occ": (o + d) % no, "vir": v}
         return [
             pltpu.make_async_remote_copy(
-                src_ref=own_v, dst_ref=own_all.at[o2], send_sem=ssem_o.at[0, d],
+                src_ref=own_in, dst_ref=own_all.at[o2], send_sem=ssem_o.at[0, d],
                 recv_sem=rsem_o.at[0, o2], device_id=peer, device_id_type=MESH),
             pltpu.make_async_remote_copy(
                 src_ref=mix.at[0], dst_ref=mix_all.at[o2], send_sem=ssem_o.at[1, d],
@@ -106,10 +122,10 @@
     def end_rows():
         return [
             pltpu.make_async_remote_copy(
-                src_ref=vir, dst_ref=vir_end, send_sem=ssem_s.at[0], recv_sem=rsem_s.at[0],
+                src_ref=vir_in, dst_ref=vir_end, send_sem=ssem_s.at[0], recv_sem=rsem_s.at[0],
                 device_id=inward, device_id_type=MESH),
             pltpu.make_async_remote_copy(
-                src_ref=keep_v, dst_ref=keep_land, send_sem=ssem_s.at[1], recv_sem=rsem_s.at[1],
+                src_ref=keep_in, dst_ref=keep_land, send_sem=ssem_s.at[1], recv_sem=rsem_s.at[1],
                 device_id=inward, device_id_type=MESH),
         ]
 
@@ -136,6 +152,9 @@
             return carry
 
         lax.fori_loop(0, no, scan_source, 0)
+        copy = pltpu.make_async_copy(nxt, order, lsem.at[6])
+        copy.start()
+        copy.wait()
 
     def group_of(d):
         return ((g + d) % ng) * 2
@@ -179,13 +198,15 @@
 
     @pl.when(is_end)
     def _():
+        own_far = z // (nz - 1) * 2 + y
+        mate_far = z // (nz - 1) * 2 + (1 - y)
         for copy in end_rows():
             copy.start()
 
         def cross(i, carry):
             @pl.when(crosses_early(i))
             def _():
-                piece(amps, v, i, ssem_g.at[2, v], side).start()
+                piece(amps, v, own_far, i, ssem_g.at[2, v], side).start()
 
             return carry
 
@@ -195,12 +216,12 @@
             ints_piece(ints, o, p, ssem_b.at[0], inward).start()
 
         def send_amps(i):
-            piece(amps, v, i, ssem_g.at[0, v], inward).start()
+            piece(amps, v, own_far, i, ssem_g.at[0, v], inward).start()
 
             @pl.when(crosses_early(i))
             def _():
-                arrive(mate, i)
-                piece(gath.at[mate], mate, i, ssem_g.at[0, mate], inward).start()
+                arrive(mate, mate_far, i)
+                piece(gath.at[mate], mate, mate_far, i, ssem_g.at[0, mate], inward).start()
 
         for p in range(nb - 1):
             send_ints(p)
@@ -243,20 +264,20 @@
                 for s in range(low + 1, high + 1):
                     flag = jnp.where(column >= s * k_tile, amp_mask[s, t].astype(jnp.float32), flag)
                 flag = jnp.broadcast_to(flag, (tr, kw)).astype(jnp.bfloat16)
-                masked[slot, n * tr:(n + 1) * tr, :] = rows_in[n * tr:(n + 1) * tr] * flag
-
-    def ladder_of(right):
+                masked[i % 2, slot, n * tr:(n + 1) * tr, :] = rows_in[n * tr:(n + 1) * tr] * flag
+
+    def ladder_of(i, right):
         if kw % 128 == 0:
-            left = jnp.concatenate([masked[slot] for slot in range(nv)], axis=1)
+            left = jnp.concatenate([masked[i % 2, slot] for slot in range(nv)], axis=1)
             return jnp.dot(left, right[...], preferred_element_type=jnp.float32)
         total = jnp.zeros((cr, cols), jnp.float32)
         for slot in range(nv):
             total += jnp.dot(
-                masked[slot], right[slot * kw:(slot + 1) * kw, :], preferred_element_type=jnp.float32)
+                masked[i % 2, slot], right[slot * kw:(slot + 1) * kw, :], preferred_element_type=jnp.float32)
         return total
 
     def update(i, right, keep_row, vir_row, store, send):
-        ladder = ladder_of(right).astype(jnp.bfloat16)
+        ladder = ladder_of(i, right).astype(jnp.bfloat16)
         for n in range(chunk_tiles):
             t = i * chunk_tiles + n
             kept = ladder[n * tr:(n + 1) * tr] * keep_row[0, t].astype(jnp.float32).astype(jnp.bfloat16)
@@ -272,70 +293,70 @@
         def send_own(i):
             @pl.when(go_up)
             def _():
-                piece(amps, v, i, ssem_g.at[0, v], above).start()
+                chunk(amps, v, i, ssem_g.at[0, v], above).start()
 
             @pl.when(go_down)
             def _():
-                piece(amps, v, i, ssem_g.at[1, v], below).start()
+                chunk(amps, v, i, ssem_g.at[1, v], below).start()
 
         def send_side(i):
-            piece(amps, v, i, ssem_g.at[2, v], side).start()
-
-        for i in range(min(ahead, np_)):
-            send_side(i)
+            chunk(amps, v, i, ssem_g.at[2, v], side).start()
 
         def all_own(i, carry):
             send_own(i)
+            send_side(i)
             return carry
 
-        lax.fori_loop(0, np_, all_own, 0)
+        lax.fori_loop(0, nc, all_own, 0)
         for d in range(1, no):
             for copy in small(d, o):
                 copy.start()
 
+        for copy in loads:
+            copy.wait()
         lanes = occ.shape[1]
         for r in range(occ.shape[0]):
             row = jnp.broadcast_to(occ[...].astype(jnp.float32)[r:r + 1], (128, lanes))
             occ_col[r * lanes:(r + 1) * lanes, :] = jnp.transpose(row)
 
-        def within(i, body):
-            @pl.when((i >= 0) & (i < np_))
+        def within(i, count, body):
+            @pl.when((i >= 0) & (i < count))
             def _():
                 body(i)
 
-        def relay(slot, i, up):
+        def relay(copy, slot, up):
             ok, sem, device = (go_up, 0, above) if up else (go_down, 1, below)
 
             @pl.when(ok)
             def _():
-                piece(gath.at[slot], slot, i, ssem_g.at[sem, slot], device).start()
+                copy(ssem_g.at[sem, slot], device).start()
 
         def from_inner(j, i):
             for near, up in ((z - j, True), (z + j, False)):
                 @pl.when((near >= 1) & (near <= nz - 2))
                 def _():
                     slot = near * 2 + y
-                    arrive(slot, i)
-                    relay(slot, i, up)
-                    piece(gath.at[slot], slot, i, ssem_g.at[2, slot], side).start()
+                    arrive_chunk(slot, i)
+                    relay(functools.partial(chunk, gath.at[slot], slot, i), slot, up)
+                    chunk(gath.at[slot], slot, i, ssem_g.at[2, slot], side).start()
 
         def from_end(j, i):
-            for near, end, up in ((z - j, 0, True), (z + j, nz - 1, False)):
+            for near, end, first, up in ((z - j, 0, 0, True), (z + j, nz - 1, 2, False)):
                 @pl.when(near == end)
                 def _():
                     slot = end * 2 + y
                     other = end * 2 + (1 - y)
-                    arrive(slot, i)
-                    relay(slot, i, up)
+                    arrive(slot, first + y, i)
+                    relay(functools.partial(piece, gath.at[slot], slot, first + y, i), slot, up)
 
                     @pl.when(crosses_early(i))
                     def _():
-                        arrive(other, i)
-                        relay(other, i, up)
+                        arrive(other, first + (1 - y), i)
+                        relay(functools.partial(piece, gath.at[other], other, first + (1 - y), i), other, up)
 
                     @pl.when(jnp.logical_not(crosses_early(i)))
                     def _():
-                        piece(gath.at[slot], slot, i, ssem_g.at[2, slot], side).start()
+                        piece(gath.at[slot], slot, first + y, i, ssem_g.at[2, slot], side).start()
 
         def from_outward(p):
             @pl.when(has_end)
@@ -363,14 +384,13 @@
             copy.wait()
 
         def compute_end(i):
+            for zz in range(1, nz - 1):
+                arrive_chunk(zz * 2 + (1 - y), i)
             for q in (2 * i, 2 * i + 1):
-                for zz in range(1, nz - 1):
-                    arrive(zz * 2 + (1 - y), q)
-
                 @pl.when(jnp.logical_not(crosses_early(q)))
                 def _():
-                    arrive(1 - y, q)
-                    arrive((nz - 1) * 2 + (1 - y), q)
+                    arrive(1 - y, 1 - y, q)
+                    arrive((nz - 1) * 2 + (1 - y), 2 + (1 - y), q)
 
             mask_rows(i)
 
@@ -399,11 +419,11 @@
         b_in = {1: (0, 1), 3: (2, 3), 5: (4, 5, 6), 7: (7,)}
         b_on = {3: (0, 1), 5: (2, 3), 6: (4, 5), 7: (6,), 9: (7,)}
         lag = 2 * (nz - 3) + 2
+        assert nz >= 4 and np_ == 2 * nc
 
         def near_part(n):
-            within(n + ahead, send_side)
             for j in range(1, nz - 2):
-                within(n - (j - 1), functools.partial(from_inner, j))
+                within(n - (j - 1), nc, functools.partial(from_inner, j))
 
         def parts_at(s, events, body):
             for at, parts in events.items():
@@ -423,7 +443,7 @@
 
         def far_part(e):
             for j in range(1, nz - 1):
-                within(e - 2 * (j - 1), functools.partial(from_end, j))
+                within(e - 2 * (j - 1), np_, functools.partial(from_end, j))
 
         def loop(low, high, body):
             def one(i, carry):
@@ -439,42 +459,27 @@
                 parts_at(s, b_on, ints_on)
 
             def early_step(e):
-                near_part(lead + e - e // 4)
+                near_part(lead + e)
                 before(lead + e)
                 far_part(e)
                 parts_at(lead + e, b_on, ints_on)
 
-            def step(e):
-                @pl.when(e % 4 != 3)
-                def _():
-                    near_part(lead + e - e // 4)
-
-                far_part(e)
 
             def pair(k):
-                step(2 * k + lag + 1)
+                far_part(2 * k + 4)
                 compute_end(k)
-                step(2 * k + lag + 2)
+                far_part(2 * k + 5)
                 compute_own(k)
 
-            def dense(k):
-                step(k + nc + lag - 3)
-                compute_end(k)
-                compute_own(k)
-
-            def closing(k):
-                step(2 * k + lag - 1)
-                compute_end(k)
-                step(2 * k + lag)
-                compute_own(k)
-
             loop(0, lead, opening)
-            loop(0, 3, early_step)
-            loop(3, 4, lambda e: (before(lead + e), far_part(e), parts_at(lead + e, b_on, ints_on)))
-            loop(4, lag + 1, step)
-            loop(0, nc - 4, pair)
-            loop(nc - 4, nc - 2, dense)
-            loop(nc - 2, nc, closing)
+            loop(0, 4, early_step)
+            loop(0, nc - 2, pair)
+            compute_end(nc - 2)
+            far_part(np_)
+            far_part(np_ + 1)
+            compute_end(nc - 1)
+            compute_own(nc - 2)
+            compute_own(nc - 1)
         else:
             def step(s):
                 near_part(s)
@@ -501,18 +506,6 @@
 
     lax.fori_loop(0, np_, last, 0)
 
-    def source(s, carry):
-        def slot(k, position):
-            t = nxt[s, position]
-            tile = tiles[s, jnp.minimum(t, td - 1)]
-            out[s * cap + k] = jnp.where(t < td, tile, jnp.zeros_like(tile))
-            return jnp.minimum(t + 1, td)
-
-        lax.fori_loop(0, cap, slot, jnp.int32(0))
-        return carry
-
-    lax.fori_loop(0, no, source, 0)
-
     def sent(whole, send_sem, recv_sem):
         pltpu.make_async_remote_copy(
             src_ref=whole, dst_ref=whole, send_sem=send_sem, recv_sem=recv_sem,
@@ -520,7 +513,7 @@
 
     def sent_rows(count, direction, slot):
         if count:
-            sent(gath.at[0, pl.ds(0, count)], ssem_g.at[direction, slot], rsem_g.at[0, 0])
+            sent(gath.at[0, pl.ds(0, count)], ssem_g.at[direction, slot], rsem_e.at[0, 0])
 
     @pl.when(is_end)
     def _():
@@ -565,6 +558,31 @@
             copy.wait_send()
 
 
+def place_kernel(cap, order, tiles, out, blank, sem):
+    no, td = tiles.shape[:2]
+    blank[...] = jnp.zeros_like(blank)
+
+    def source(s, carry):
+        def slot(k, position):
+            t = order[s, position]
+
+            @pl.when(t < td)
+            def _():
+                pltpu.make_async_copy(tiles.at[s, t], out.at[s * cap + k], sem).start()
+
+            @pl.when(t >= td)
+            def _():
+                pltpu.make_async_copy(blank, out.at[s * cap + k], sem).start()
+
+            return jnp.minimum(t + 1, td)
+
+        lax.fori_loop(0, cap, slot, jnp.int32(0))
+        return carry
+
+    lax.fori_loop(0, no, source, 0)
+    pltpu.make_async_copy(out, out, sem).wait()
+
+
 def shards(no, nv, amps, ints, amp_mask, keep_mask, owners, occ_energy, vir_energy, mix):
     td, k_tiles = amp_mask.shape
     rows, kw = amps.shape
@@ -575,8 +593,8 @@
     chunk_tiles = max(1, min(td, 128 // tr))
     nc = td // chunk_tiles
     pieces = 2 * nc
-    ahead, lead, nb, late = 4, 6, 8, 3 * pieces // 4
-    cfg = (no, nv, td, tr, chunk_tiles, k_tile, ahead, lead, nb, late)
+    lead, nb, late = 6, 8, 3 * pieces // 8
+    cfg = (no, nv, td, tr, chunk_tiles, k_tile, lead, nb, late)
     smem = pl.BlockSpec(memory_space=pltpu.SMEM)
     vmem = pl.BlockSpec(memory_space=pltpu.VMEM)
     hbm = pl.BlockSpec(memory_space=pl.ANY)
@@ -584,18 +602,26 @@
     own = owners.reshape(1, td)
     keep = keep_mask.reshape(1, td)
     dma = pltpu.SemaphoreType.DMA
-    return pl.pallas_call(
+    room = (63 << 20) - no * td * tr * cols * 2
+    tiles, order = pl.pallas_call(
         functools.partial(ladder_kernel, cfg),
-        out_shape=jax.ShapeDtypeStruct((no * cap, tr, cols), jnp.bfloat16),
-        in_specs=[hbm, hbm, smem, smem, smem, vmem, vmem, vmem, vmem, vmem],
-        out_specs=vmem,
+        out_shape=(
+            pltpu.VMEM((no, td, tr, cols), jnp.bfloat16),
+            pltpu.VMEM((no, td + 1), jnp.int32),
+        ),
+        in_specs=[hbm] * 8,
+        out_specs=(vmem, hbm),
         scratch_shapes=[
+            pltpu.SMEM((k_tiles, td), jnp.int32),
+            pltpu.SMEM((1, td), jnp.int32),
+            pltpu.SMEM((1, td), jnp.int32),
+            pltpu.VMEM((rows // 128, 128), jnp.bfloat16),
+            pltpu.VMEM((1, cols), jnp.float32),
             pltpu.VMEM((nv, rows, kw), jnp.bfloat16),
             pltpu.VMEM(ints.shape, jnp.bfloat16),
             pltpu.VMEM(ints.shape, jnp.bfloat16),
-            pltpu.VMEM((nv, chunk_tiles * tr, kw), jnp.bfloat16),
+            pltpu.VMEM((2, nv, chunk_tiles * tr, kw), jnp.bfloat16),
             pltpu.VMEM((rows, 128), jnp.float32),
-            pltpu.VMEM((no, td, tr, cols), jnp.bfloat16),
             pltpu.VMEM((td, tr, cols), jnp.bfloat16),
             pltpu.VMEM((no, tr, tr), jnp.bfloat16),
             pltpu.VMEM((no, 1, td), jnp.int32),
@@ -604,8 +630,9 @@
             pltpu.VMEM((1, cols), jnp.float32),
             pltpu.VMEM((1, td), jnp.int32),
             pltpu.SMEM((1, td), jnp.int32),
-            dma((6,)),
-            dma((nv, pieces)),
+            dma((12,)),
+            dma((nv - 4, nc)),
+            dma((4, pieces)),
             dma((3, nv)),
             dma((no, nb)),
             dma((1,)),
@@ -621,13 +648,20 @@
             dma((2,)),
         ],
         compiler_params=pltpu.CompilerParams(
-            collective_id=0, has_side_effects=True, vmem_limit_bytes=60 * 1024 * 1024
+            collective_id=0, has_side_effects=True, vmem_limit_bytes=room
         ),
     )(
-        amps, ints, amp_mask.T, keep, own, own,
-        occ_energy.reshape(rows // 128, 128),
-        vir_energy.reshape(1, cols), mix, keep,
+        amps, ints, amp_mask.T, keep, own, occ_energy.reshape(rows // 128, 128),
+        vir_energy.reshape(1, cols), mix,
     )
+    return pl.pallas_call(
+        functools.partial(place_kernel, cap),
+        out_shape=jax.ShapeDtypeStruct((no * cap, tr, cols), jnp.bfloat16),
+        in_specs=[smem, vmem],
+        out_specs=hbm,
+        scratch_shapes=[pltpu.VMEM((tr, cols), jnp.bfloat16), dma],
+        compiler_params=pltpu.CompilerParams(vmem_limit_bytes=24 * 1024 * 1024),
+    )(order, tiles)
 
 
 def solution(mesh):

time: 76.6 us -> 71.7 us (0.936)
  local copies, waits for them, and re-layouts: 3.16 us -> 0 us
  Pallas kernels: 72.8 us -> 71.5 us
    unnamed x1 -> x0, local copies, waits for them, and re-layouts: 3.16 us -> none
    pallas_call x1 -> x2, Pallas kernels: 72.8 us -> 71.5 us  [the longest x1 69.5 us: shards(): pl.pallas_call(functools.partial(ladder_kernel, cfg), out_shape=(pltpu.VM...]
where the time goes in v3:
time: 71.7 us; the launch traced here: 71.5 us
  Pallas kernels  71.5 us (100%)
    pallas_call x1, Pallas kernels, shards(): pl.pallas_call(functools.partial(ladder_kernel, cfg), out_shape=(pltpu.VM...  69.5 us
    pallas_call x1, Pallas kernels, shards(): pl.pallas_call(functools.partial(place_kernel, cap), out_shape=jax.ShapeD...  2.03 us

profile of v3, /device:TPU:0, one launch (start us, length us, event | category | flops | bytes accessed | tf_op | source)
XLA Modules:
  0.0 71.5 jit_solution(13654076157475092480)
XLA Ops:
  0.0 69.5 %shard_map.82 = (bf16[4,32,32,512]{3,2,1,0:T(8,128)(2,1)S(1)}, s32[4,33]{1,0:T(4,128)S(1)}) custom-call(bf16[1024,384]{1,0:T(8,128)(2,1)} %amps.1, bf16[3072,512]{1,0:T(8,128)(2,1)} %ints.1, s32[6,32]{1,0:T(8,128)} %bitcast.5, s32[1,32]{1,0:T(1,128)} %bitcast.8, s32[1,32]{1,0:T(1,128)} %bitcast.9, bf16[8,128]{1,0:T(8,128)(2,1)} %bitcast.6, ...), custom_call_target="tpu_custom_call" | custom-call | tf_op jit(solution)/shard_map/pallas_call | solution.py:606
  69.5 2.0 %shard_map.83 = bf16[64,32,512]{2,1,0:T(8,128)(2,1)} custom-call(s32[4,33]{1,0:T(4,128)S(1)} %get-tuple-element.7.order, bf16[4,32,32,512]{3,2,1,0:T(8,128)(2,1)S(1)} %get-tuple-element.8.tiles), custom_call_target="tpu_custom_call" | custom-call | tf_op jit(solution)/shard_map/pallas_call | solution.py:657

commit v4 on v3

--- a/solution.py
+++ b/solution.py
@@ -1,4 +1,5 @@
 import functools
+import operator
 
 import jax
 import jax.numpy as jnp
@@ -83,10 +84,15 @@
     both = jnp.where(z < nz - 1, 1, 0) + jnp.where(z > 0, 1, 0)
     pl.semaphore_wait(barrier, no + both)
 
+    at_both, at_first = late if nz == 4 else (late[0], ())
+
+    def among(i, pieces):
+        return functools.reduce(operator.or_, [i == q for q in pieces], i < 0)
+
     def crosses_early(i):
-        return (i < late) | (i >= late + np_ // 2) | (i % 2 == 1)
-
-    early = sum(1 for i in range(np_) if i < late or i >= late + np_ // 2 or i % 2 == 1) * pr
+        return jnp.logical_not(among(i, at_both + at_first))
+
+    early = (np_ - len(at_both) - len(at_first)) * pr
 
     def piece(src, slot, far, i, send_sem, device):
         window = pl.ds(pl.multiple_of(i * pr, pr), pr)
@@ -159,15 +165,20 @@
     def group_of(d):
         return ((g + d) % ng) * 2
 
+    def tile_window(p):
+        if isinstance(p, int) and p >= nc - 1:
+            return pl.ds((nc - 1) * chunk_tiles + (p - nc + 1) * pt, pt)
+        return pl.ds(p * chunk_tiles, chunk_tiles)
+
     def tile_piece(o2, i, send_sem, device):
-        window = pl.ds(i * pt, pt)
+        window = tile_window(i)
         return pltpu.make_async_remote_copy(
             src_ref=tiles.at[o2, window], dst_ref=tiles.at[o2, window], send_sem=send_sem,
             recv_sem=rsem_t.at[o2, i], device_id=device, device_id_type=MESH,
         )
 
     def back_piece(i):
-        window = pl.ds(i * pt, pt)
+        window = tile_window(i)
         return pltpu.make_async_remote_copy(
             src_ref=tiles_end.at[window], dst_ref=tiles.at[o, window], send_sem=ssem_r.at[0],
             recv_sem=rsem_t.at[o, i], device_id=outward, device_id_type=MESH,
@@ -238,55 +249,69 @@
         lax.fori_loop(1, np_, rest, 0)
         table()
 
-        def pass_on(i, carry):
+        def pass_on(i):
             tile_piece(o, i, ssem_c.at[0], partner).wait_recv()
             share_out(i)
 
-            @pl.when(i >= 3)
-            def _():
-                hand_on(i - 3)
+        def passing(i, carry):
+            pass_on(i)
+
+            @pl.when(i >= 2)
+            def _():
+                hand_on(i - 2)
 
             return carry
 
-        lax.fori_loop(0, np_, pass_on, 0)
-        for i in range(np_ - 3, np_):
+        lax.fori_loop(0, nc - 1, passing, 0)
+        for i in (nc - 1, nc):
+            pass_on(i)
+            hand_on(i - 2)
+        for i in (nc - 1, nc):
             hand_on(i)
 
-    def mask_rows(i):
-        first = pl.multiple_of(i * cr, cr)
+    def mask_rows(i, tiles_in):
+        first = pl.multiple_of(i * cr + tiles_in[0] * tr, tr)
         for slot in range(nv):
-            rows_in = gath[slot, pl.ds(first, cr), :]
+            rows_in = gath[slot, pl.ds(first, len(tiles_in) * tr), :]
             column = slot * kw + lax.broadcasted_iota(jnp.int32, (1, kw), 1)
             low, high = slot * kw // k_tile, ((slot + 1) * kw - 1) // k_tile
-            for n in range(chunk_tiles):
+            for place, n in enumerate(tiles_in):
                 t = i * chunk_tiles + n
                 flag = jnp.full((1, kw), amp_mask[low, t].astype(jnp.float32))
                 for s in range(low + 1, high + 1):
                     flag = jnp.where(column >= s * k_tile, amp_mask[s, t].astype(jnp.float32), flag)
                 flag = jnp.broadcast_to(flag, (tr, kw)).astype(jnp.bfloat16)
-                masked[i % 2, slot, n * tr:(n + 1) * tr, :] = rows_in[n * tr:(n + 1) * tr] * flag
-
-    def ladder_of(i, right):
+                masked[i % 2, slot, n * tr:(n + 1) * tr, :] = rows_in[place * tr:(place + 1) * tr] * flag
+
+    def ladder_of(i, tiles_in, right):
+        held = pl.ds(tiles_in[0] * tr, len(tiles_in) * tr)
         if kw % 128 == 0:
-            left = jnp.concatenate([masked[i % 2, slot] for slot in range(nv)], axis=1)
+            left = jnp.concatenate([masked[i % 2, slot, held, :] for slot in range(nv)], axis=1)
             return jnp.dot(left, right[...], preferred_element_type=jnp.float32)
-        total = jnp.zeros((cr, cols), jnp.float32)
+        total = jnp.zeros((len(tiles_in) * tr, cols), jnp.float32)
         for slot in range(nv):
             total += jnp.dot(
-                masked[i % 2, slot], right[slot * kw:(slot + 1) * kw, :], preferred_element_type=jnp.float32)
+                masked[i % 2, slot, held, :], right[slot * kw:(slot + 1) * kw, :],
+                preferred_element_type=jnp.float32)
         return total
 
-    def update(i, right, keep_row, vir_row, store, send):
-        ladder = ladder_of(i, right).astype(jnp.bfloat16)
-        for n in range(chunk_tiles):
+    every = range(chunk_tiles)
+    halves = [range(h * pt, (h + 1) * pt) for h in range(2)]
+
+    def update(i, tiles_in, right, keep_row, vir_row, store, send):
+        ladder = ladder_of(i, tiles_in, right).astype(jnp.bfloat16)
+        for place, n in enumerate(tiles_in):
             t = i * chunk_tiles + n
-            kept = ladder[n * tr:(n + 1) * tr] * keep_row[0, t].astype(jnp.float32).astype(jnp.bfloat16)
+            kept = ladder[place * tr:(place + 1) * tr] * keep_row[0, t].astype(jnp.float32).astype(jnp.bfloat16)
             mixed = jnp.dot(mix_all[own_s[0, t]], kept, preferred_element_type=jnp.float32)
             energy = occ_col[pl.ds(pl.multiple_of(t * tr, tr), tr), :]
             denominator = vir_row[...] - jnp.concatenate([energy] * (cols // 128), axis=1)
             store(t, (mixed / denominator).astype(jnp.bfloat16))
-            if n % pt == pt - 1:
-                send(2 * i + n // pt)
+            if isinstance(i, int) and i == nc - 1:
+                if n % pt == pt - 1:
+                    send(i + n // pt)
+            elif n == chunk_tiles - 1:
+                send(i)
 
     @pl.when(inner)
     def _():
@@ -377,47 +402,59 @@
             for p in range(nb):
                 for d in range(ng):
                     ints_arrive(group_of(d) + (1 - c), p)
-            for copy in end_rows():
-                copy.wait_recv()
-            copy = pltpu.make_async_copy(keep_land, keep_end, lsem.at[5])
-            copy.start()
-            copy.wait()
-
-        def compute_end(i):
-            for zz in range(1, nz - 1):
-                arrive_chunk(zz * 2 + (1 - y), i)
-            for q in (2 * i, 2 * i + 1):
-                @pl.when(jnp.logical_not(crosses_early(q)))
-                def _():
-                    arrive(1 - y, 1 - y, q)
-                    arrive((nz - 1) * 2 + (1 - y), 2 + (1 - y), q)
-
-            mask_rows(i)
+
+        def compute_end(i, tiles_in=every):
+            if tiles_in[0] == 0:
+                for zz in range(1, nz - 1):
+                    arrive_chunk(zz * 2 + (1 - y), i)
+            for q in range(2 * i + tiles_in[0] // pt, 2 * i + tiles_in[-1] // pt + 1) if isinstance(i, int) else (2 * i, 2 * i + 1):
+                if nz == 4:
+                    near, far = z - 1, 2 - z
+
+                    @pl.when(among(q, at_both))
+                    def _():
+                        arrive(near * 6 + 1 - y, near * 2 + 1 - y, q)
+
+                    @pl.when(jnp.logical_not(among(q, at_both)))
+                    def _():
+                        arrive(far * 6 + y, far * 2 + y, q)
+
+                    arrive(far * 6 + 1 - y, far * 2 + 1 - y, q)
+                else:
+                    @pl.when(jnp.logical_not(crosses_early(q)))
+                    def _():
+                        arrive(1 - y, 1 - y, q)
+                        arrive((nz - 1) * 2 + (1 - y), 2 + (1 - y), q)
+
+            mask_rows(i, tiles_in)
 
             @pl.when(has_end)
             def _():
-                @pl.when(i == 0)
-                def _():
-                    ints_last()
+                if not (isinstance(i, int) and i):
+                    @pl.when(i == 0)
+                    def _():
+                        ints_last()
 
                 def store_end(t, value):
                     tiles_end[t] = value
 
-                update(i, ints_end, keep_end, vir_end, store_end, lambda q: back_piece(q).start())
+                update(i, tiles_in, ints_end, keep_end, vir_end, store_end, lambda q: back_piece(q).start())
 
         def compute_own(i):
             def store_own(t, value):
                 tiles[o, t] = value
 
-            update(i, ints_own, keep, vir, store_own, share_out)
-
-            @pl.when(i >= 2)
-            def _():
-                hand_on(2 * i - 4)
-                hand_on(2 * i - 3)
-
-        b_in = {1: (0, 1), 3: (2, 3), 5: (4, 5, 6), 7: (7,)}
-        b_on = {3: (0, 1), 5: (2, 3), 6: (4, 5), 7: (6,), 9: (7,)}
+            update(i, every, ints_own, keep, vir, store_own, share_out)
+
+            if isinstance(i, int):
+                hand_on(i - 2)
+            else:
+                @pl.when(i >= 2)
+                def _():
+                    hand_on(i - 2)
+
+        b_in = {0: (0,), 1: (1,), 2: (2,), 3: (3,), 4: (4,), 5: (5,), 6: (6,), 7: (7,)}
+        b_on = {3: (0,), 4: (1,), 5: (2,), 6: (3,), 7: (4, 5), 8: (6, 7)}
         lag = 2 * (nz - 3) + 2
         assert nz >= 4 and np_ == 2 * nc
 
@@ -441,7 +478,58 @@
                 load_amps.wait()
                 table()
 
+                @pl.when(has_end)
+                def _():
+                    for copy in end_rows():
+                        copy.wait_recv()
+                    copy = pltpu.make_async_copy(keep_land, keep_end, lsem.at[5])
+                    copy.start()
+                    copy.wait()
+
+        def ends_part(e):
+            near, far = z - 1, 2 - z
+            across = {"occ": o, "vir": (3 - z) * 2 + y}
+
+            def to_across(slot, far_slot, i):
+                piece(gath.at[slot], slot, far_slot, i, ssem_g.at[near, slot], across).start()
+
+            def to_side(slot, far_slot, i):
+                piece(gath.at[slot], slot, far_slot, i, ssem_g.at[2, slot], side).start()
+
+            def first(i):
+                slot, other = near * 6 + y, near * 6 + 1 - y
+                arrive(slot, near * 2 + y, i)
+                to_across(slot, near * 2 + y, i)
+
+                @pl.when(crosses_early(i))
+                def _():
+                    arrive(other, near * 2 + 1 - y, i)
+                    to_across(other, near * 2 + 1 - y, i)
+
+                @pl.when(jnp.logical_not(crosses_early(i)))
+                def _():
+                    to_side(slot, near * 2 + y, i)
+
+            def second(i):
+                slot, other = far * 6 + y, near * 6 + 1 - y
+
+                @pl.when(among(i, at_both))
+                def _():
+                    arrive(slot, far * 2 + y, i)
+                    to_side(slot, far * 2 + y, i)
+
+                @pl.when(among(i, at_first))
+                def _():
+                    arrive(other, near * 2 + 1 - y, i)
+                    to_across(other, near * 2 + 1 - y, i)
+
+            within(e, np_, first)
+            within(e - 2, np_, second)
+
         def far_part(e):
+            if nz == 4:
+                ends_part(e)
+                return
             for j in range(1, nz - 1):
                 within(e - 2 * (j - 1), np_, functools.partial(from_end, j))
 
@@ -475,10 +563,9 @@
             loop(0, 4, early_step)
             loop(0, nc - 2, pair)
             compute_end(nc - 2)
-            far_part(np_)
-            far_part(np_ + 1)
-            compute_end(nc - 1)
             compute_own(nc - 2)
+            for half in halves:
+                compute_end(nc - 1, half)
             compute_own(nc - 1)
         else:
             def step(s):
@@ -488,15 +575,17 @@
                 far_part(e)
                 parts_at(s, b_on, ints_on)
 
-                @pl.when((e > lag) & ((e - lag) % 2 == 1) & (e < lag + 2 * nc))
+                @pl.when((e > lag) & ((e - lag) % 2 == 1) & (e < lag + 2 * nc - 2))
                 def _():
                     k = (e - lag - 1) // 2
                     compute_end(k)
                     compute_own(k)
 
             loop(0, lead + np_ + lag, step)
-
-        for i in range(np_ - 4, np_):
+            compute_end(nc - 1)
+            compute_own(nc - 1)
+
+        for i in (nc - 2, nc - 1, nc):
             hand_on(i)
 
     def last(i, carry):
@@ -504,7 +593,9 @@
             tile_piece(group_of(d) + (1 - c), i, ssem_c.at[d], partner).wait_recv()
         return carry
 
-    lax.fori_loop(0, np_, last, 0)
+    lax.fori_loop(0, nc - 1, last, 0)
+    for i in (nc - 1, nc):
+        last(i, 0)
 
     def sent(whole, send_sem, recv_sem):
         pltpu.make_async_remote_copy(
@@ -534,11 +625,16 @@
                 def _():
                     sent_rows(rows, direction, zz * 2 + y)
                     if is_far:
-                        sent_rows(early, direction, zz * 2 + (1 - y))
+                        sent_rows(early + len(at_first) * pr, direction, zz * 2 + (1 - y))
 
             @pl.when(zz != z)
             def _():
-                sent_rows(rows - early if is_far else rows, 2, zz * 2 + y)
+                sent_rows(len(at_both) * pr if is_far else rows, 2, zz * 2 + y)
+
+            if is_far and at_first:
+                @pl.when(z == (1 if zz == 0 else nz - 2))
+                def _():
+                    sent_rows(len(at_first) * pr, 2, zz * 2 + y)
 
         @pl.when(has_end)
         def _():
@@ -593,7 +689,7 @@
     chunk_tiles = max(1, min(td, 128 // tr))
     nc = td // chunk_tiles
     pieces = 2 * nc
-    lead, nb, late = 6, 8, 3 * pieces // 8
+    lead, nb, late = 6, 8, ((6, 8, 10, 12), ())
     cfg = (no, nv, td, tr, chunk_tiles, k_tile, lead, nb, late)
     smem = pl.BlockSpec(memory_space=pltpu.SMEM)
     vmem = pl.BlockSpec(memory_space=pltpu.VMEM)
@@ -638,7 +734,7 @@
             dma((1,)),
             dma((ng,)),
             dma((ng,)),
-            dma((no, pieces)),
+            dma((no, nc + 1)),
             dma((ng,)),
             dma((ng,)),
             dma((1,)),

time: 71.7 us -> 71.1 us (level)
  no operation moved by 1% of the time
where the time goes in v4:
time: 71.1 us; the launch traced here: 70.9 us
  Pallas kernels  70.9 us (100%)
    pallas_call x1, Pallas kernels, shards(): pl.pallas_call(functools.partial(ladder_kernel, cfg), out_shape=(pltpu.VM...  68.9 us
    pallas_call x1, Pallas kernels, shards(): pl.pallas_call(functools.partial(place_kernel, cap), out_shape=jax.ShapeD...  2.03 us

profile of v4, /device:TPU:0, one launch (start us, length us, event | category | flops | bytes accessed | tf_op | source)
XLA Modules:
  0.0 70.9 jit_solution(14939835431820579575)
XLA Ops:
  0.0 68.9 %shard_map.82 = (bf16[4,32,32,512]{3,2,1,0:T(8,128)(2,1)S(1)}, s32[4,33]{1,0:T(4,128)S(1)}) custom-call(bf16[1024,384]{1,0:T(8,128)(2,1)} %amps.1, bf16[3072,512]{1,0:T(8,128)(2,1)} %ints.1, s32[6,32]{1,0:T(8,128)} %bitcast.5, s32[1,32]{1,0:T(1,128)} %bitcast.8, s32[1,32]{1,0:T(1,128)} %bitcast.9, bf16[8,128]{1,0:T(8,128)(2,1)} %bitcast.6, ...), custom_call_target="tpu_custom_call" | custom-call | tf_op jit(solution)/shard_map/pallas_call | solution.py:702
  68.9 2.0 %shard_map.83 = bf16[64,32,512]{2,1,0:T(8,128)(2,1)} custom-call(s32[4,33]{1,0:T(4,128)S(1)} %get-tuple-element.7.order, bf16[4,32,32,512]{3,2,1,0:T(8,128)(2,1)S(1)} %get-tuple-element.8.tiles), custom_call_target="tpu_custom_call" | custom-call | tf_op jit(solution)/shard_map/pallas_call | solution.py:753

commit v5 on v4

--- a/solution.py
+++ b/solution.py
@@ -13,7 +13,7 @@
 
 def ladder_kernel(
     cfg, amps, ints, amp_mask_in, keep_in, own_in, occ_in, vir_in, mix, tiles, order,
-    amp_mask, keep, own_s, occ, vir, gath, ints_own, ints_end, masked, occ_col, tiles_end, mix_all, own_all, own_tab, nxt,
+    amp_mask, keep, own_s, occ, vir, gath, ints_own, ints_end, masked, occ_col, tiles_end, mix_all, own_all, own_tab, nxt, placed,
     vir_end, keep_land, keep_end,
     lsem, rsem_n, rsem_e, ssem_g, rsem_b, ssem_b, ssem_bx, ssem_bc, rsem_t, ssem_c, ssem_t, ssem_r,
     rsem_o, ssem_o, rsem_s, ssem_s,
@@ -155,10 +155,17 @@
                 return following
 
             lax.fori_loop(0, td, back, jnp.int32(td))
+
+            def place(k, position):
+                t = nxt[s, position]
+                placed[s, k] = t
+                return jnp.minimum(t + 1, td)
+
+            lax.fori_loop(0, order.shape[1], place, jnp.int32(0))
             return carry
 
         lax.fori_loop(0, no, scan_source, 0)
-        copy = pltpu.make_async_copy(nxt, order, lsem.at[6])
+        copy = pltpu.make_async_copy(placed, order, lsem.at[6])
         copy.start()
         copy.wait()
 
@@ -265,8 +272,7 @@
         lax.fori_loop(0, nc - 1, passing, 0)
         for i in (nc - 1, nc):
             pass_on(i)
-            hand_on(i - 2)
-        for i in (nc - 1, nc):
+        for i in (nc - 3, nc - 2, nc - 1, nc):
             hand_on(i)
 
     def mask_rows(i, tiles_in):
@@ -447,7 +453,8 @@
             update(i, every, ints_own, keep, vir, store_own, share_out)
 
             if isinstance(i, int):
-                hand_on(i - 2)
+                if i >= 2:
+                    hand_on(i - 2)
             else:
                 @pl.when(i >= 2)
                 def _():
@@ -659,8 +666,8 @@
     blank[...] = jnp.zeros_like(blank)
 
     def source(s, carry):
-        def slot(k, position):
-            t = order[s, position]
+        for k in range(cap):
+            t = order[s, k]
 
             @pl.when(t < td)
             def _():
@@ -670,9 +677,6 @@
             def _():
                 pltpu.make_async_copy(blank, out.at[s * cap + k], sem).start()
 
-            return jnp.minimum(t + 1, td)
-
-        lax.fori_loop(0, cap, slot, jnp.int32(0))
         return carry
 
     lax.fori_loop(0, no, source, 0)
@@ -703,7 +707,7 @@
         functools.partial(ladder_kernel, cfg),
         out_shape=(
             pltpu.VMEM((no, td, tr, cols), jnp.bfloat16),
-            pltpu.VMEM((no, td + 1), jnp.int32),
+            pltpu.VMEM((no, cap), jnp.int32),
         ),
         in_specs=[hbm] * 8,
         out_specs=(vmem, hbm),
@@ -723,6 +727,7 @@
             pltpu.VMEM((no, 1, td), jnp.int32),
             pltpu.SMEM((no, 1, td), jnp.int32),
             pltpu.SMEM((no, td + 1), jnp.int32),
+            pltpu.SMEM((no, cap), jnp.int32),
             pltpu.VMEM((1, cols), jnp.float32),
             pltpu.VMEM((1, td), jnp.int32),
             pltpu.SMEM((1, td), jnp.int32),

time: 71.1 us -> 70.8 us (level)
  no operation moved by 1% of the time
where the time goes in v5:
time: 70.8 us; the launch traced here: 70.6 us
  Pallas kernels  70.6 us (100%)
    pallas_call x1, Pallas kernels, shards(): pl.pallas_call(functools.partial(ladder_kernel, cfg), out_shape=(pltpu.VM...  68.8 us
    pallas_call x1, Pallas kernels, shards(): pl.pallas_call(functools.partial(place_kernel, cap), out_shape=jax.ShapeD...  1.86 us

profile of v5, /device:TPU:0, one launch (start us, length us, event | category | flops | bytes accessed | tf_op | source)
XLA Modules:
  0.0 70.6 jit_solution(3421983517649748869)
XLA Ops:
  0.0 68.8 %shard_map.82 = (bf16[4,32,32,512]{3,2,1,0:T(8,128)(2,1)S(1)}, s32[4,16]{1,0:T(4,128)S(1)}) custom-call(bf16[1024,384]{1,0:T(8,128)(2,1)} %amps.1, bf16[3072,512]{1,0:T(8,128)(2,1)} %ints.1, s32[6,32]{1,0:T(8,128)} %bitcast.5, s32[1,32]{1,0:T(1,128)} %bitcast.8, s32[1,32]{1,0:T(1,128)} %bitcast.9, bf16[8,128]{1,0:T(8,128)(2,1)} %bitcast.6, ...), custom_call_target="tpu_custom_call" | custom-call | tf_op jit(solution)/shard_map/pallas_call | solution.py:706
  68.8 1.9 %shard_map.83 = bf16[64,32,512]{2,1,0:T(8,128)(2,1)} custom-call(s32[4,16]{1,0:T(4,128)S(1)} %get-tuple-element.7.order, bf16[4,32,32,512]{3,2,1,0:T(8,128)(2,1)S(1)} %get-tuple-element.8.tiles), custom_call_target="tpu_custom_call" | custom-call | tf_op jit(solution)/shard_map/pallas_call | solution.py:758

commit v6 on v5

--- a/solution.py
+++ b/solution.py
@@ -693,7 +693,7 @@
     chunk_tiles = max(1, min(td, 128 // tr))
     nc = td // chunk_tiles
     pieces = 2 * nc
-    lead, nb, late = 6, 8, ((6, 8, 10, 12), ())
+    lead, nb, late = 6, 8, ((6, 8, 9, 10), ())
     cfg = (no, nv, td, tr, chunk_tiles, k_tile, lead, nb, late)
     smem = pl.BlockSpec(memory_space=pltpu.SMEM)
     vmem = pl.BlockSpec(memory_space=pltpu.VMEM)

time: 70.8 us -> 70.7 us (level)
  no operation moved by 1% of the time
where the time goes in v6:
time: 70.7 us; the launch traced here: 70.5 us
  Pallas kernels  70.5 us (100%)
    pallas_call x1, Pallas kernels, shards(): pl.pallas_call(functools.partial(ladder_kernel, cfg), out_shape=(pltpu.VM...  68.7 us
    pallas_call x1, Pallas kernels, shards(): pl.pallas_call(functools.partial(place_kernel, cap), out_shape=jax.ShapeD...  1.86 us

profile of v6, /device:TPU:0, one launch (start us, length us, event | category | flops | bytes accessed | tf_op | source)
XLA Modules:
  0.0 70.5 jit_solution(15031433848555819324)
XLA Ops:
  0.0 68.7 %shard_map.82 = (bf16[4,32,32,512]{3,2,1,0:T(8,128)(2,1)S(1)}, s32[4,16]{1,0:T(4,128)S(1)}) custom-call(bf16[1024,384]{1,0:T(8,128)(2,1)} %amps.1, bf16[3072,512]{1,0:T(8,128)(2,1)} %ints.1, s32[6,32]{1,0:T(8,128)} %bitcast.5, s32[1,32]{1,0:T(1,128)} %bitcast.8, s32[1,32]{1,0:T(1,128)} %bitcast.9, bf16[8,128]{1,0:T(8,128)(2,1)} %bitcast.6, ...), custom_call_target="tpu_custom_call" | custom-call | tf_op jit(solution)/shard_map/pallas_call | solution.py:706
  68.7 1.9 %shard_map.83 = bf16[64,32,512]{2,1,0:T(8,128)(2,1)} custom-call(s32[4,16]{1,0:T(4,128)S(1)} %get-tuple-element.7.order, bf16[4,32,32,512]{3,2,1,0:T(8,128)(2,1)S(1)} %get-tuple-element.8.tiles), custom_call_target="tpu_custom_call" | custom-call | tf_op jit(solution)/shard_map/pallas_call | solution.py:758
